TPU v7x, 32 devices: a whole 2x2x4 slice. The times are simulated.
32 devices in a mesh: gx: 4 (over y, core), gy: 4 (over z), ha: 2 (over x).
Axes of the slice: x: 2, y: 2, z: 4, core: 2. Of those that a mesh axis runs over, the one named last changes fastest.
Arguments:
- value: float32 [4, 16, 32, 512], P(None, 'ha', 'gy', 'gx'), may hold values from -6 to 6
- obstacles: float32 [5, 128], replicated, may hold values from -1 to 1
- obstacle_slots: int32 [4, 16], P('ha'), may hold values from 0 to 127
- horizon: float32 [1], replicated, may hold values from 0.5 to 2
- speed_offset: int32 [1], replicated, may hold values from 2 to 11
Outputs:
- next_value: float32 [4, 16, 32, 512], P(None, 'ha', 'gy', 'gx')
Inputs may be any that keep to these rules, and one draw needn't show every extreme that they name: `obstacle_slots`: each heading group of 4 headings lists 16 obstacle numbers, repeats allowed.
All inputs are finite; a program needn't handle non-finite values.
Results may differ from a plain program's by a relative error of at most 0.00002.
Values sent between devices are 32-bit elements; how exact they have to be, the bound alone decides.
No kernel may reach another device: no remote copies, remote signals or barrier semaphores. Data moves between devices by JAX's collectives and lax.ppermute only.
A program may use at most 64 MiB of HBM per device.

v0:
```python
import math

import jax
import jax.numpy as jnp
from jax import lax
from jax.sharding import PartitionSpec as P

GH = 4


cfl_number = 0.75
weno_eps = 1e-06
half_width = 20.0
speed_step = 0.5
turn_limit = 1.0
accel_limit = 4.0
obstacle_speed = 2.0
car_radius = 0.8
body_offsets = (-1.0, 0.0, 1.0)


def extended_2(value, sides, width, wrap):
    for axis, dim in sides:
        count, length = (lax.axis_size(axis), value.shape[dim])
        up = [(i, (i + 1) % count) for i in range(count if wrap else count - 1)]
        down = [(j, i) for i, j in up]
        last = lax.slice_in_dim(value, length - width, length, axis=dim)
        initial = lax.slice_in_dim(value, 0, width, axis=dim)
        before = lax.ppermute(last, axis, up)
        after = lax.ppermute(initial, axis, down)
        value = jnp.concatenate([before, value, after], axis=dim)
    return value


def weno_side(outer_diff, middle_diff, inner_diff):
    weight_one = 1.0 / 3.0 / jnp.square(weno_eps + jnp.square(middle_diff - outer_diff))
    weight_two = 2.0 / 3.0 / jnp.square(weno_eps + jnp.square(inner_diff - middle_diff))
    return (
        weight_one * (1.5 * middle_diff - 0.5 * outer_diff)
        + weight_two * (0.5 * middle_diff + 0.5 * inner_diff)
    ) / (weight_one + weight_two)


def slopes(padded, along_dim, spacing):
    length = padded.shape[along_dim] - 4
    samples = [
        lax.slice_in_dim(padded, offset_idx, offset_idx + length, axis=along_dim)
        for offset_idx in range(5)
    ]
    back_far = (samples[1] - samples[0]) / spacing
    back_near = (samples[2] - samples[1]) / spacing
    ahead_near = (samples[3] - samples[2]) / spacing
    ahead_far = (samples[4] - samples[3]) / spacing
    return (weno_side(back_far, back_near, ahead_near), weno_side(ahead_far, ahead_near, back_near))


def hamiltonian_rate(pieces, speeds, angles, spreads, spacings):
    speed_minus, speed_plus = slopes(pieces[0], 0, spacings[0])
    head_minus, head_plus = slopes(pieces[1], 1, spacings[1])
    y_minus, y_plus = slopes(pieces[2], 2, spacings[2])
    x_minus, x_plus = slopes(pieces[3], 3, spacings[3])
    along_x = speeds[:, None, None, None] * jnp.cos(angles)[None, :, None, None]
    along_y = speeds[:, None, None, None] * jnp.sin(angles)[None, :, None, None]
    hamilton = along_x * (0.5 * (x_minus + x_plus)) + along_y * (0.5 * (y_minus + y_plus))
    hamilton = (
        hamilton
        + turn_limit * jnp.abs(0.5 * (head_minus + head_plus))
        + accel_limit * jnp.abs(0.5 * (speed_minus + speed_plus))
    )
    damping = spreads[0] * (x_plus - x_minus) + spreads[1] * (y_plus - y_minus)
    damping = (
        damping + turn_limit * (head_plus - head_minus) + accel_limit * (speed_plus - speed_minus)
    )
    return jnp.minimum(0.0, hamilton - 0.5 * damping)


def speed_bounds(speeds, angles, step_x, step_y):
    along_x = jnp.abs(speeds[:, None] * jnp.cos(angles)[None, :])
    along_y = jnp.abs(speeds[:, None] * jnp.sin(angles)[None, :])
    return (jnp.max(along_x), jnp.max(along_y), jnp.max(along_x / step_x + along_y / step_y))


def group_field(obstacles, horizon, step_time, x_cells, y_cells, angle_group, slot_row):
    moment = horizon[0] + step_time
    centre_x = half_width * obstacles[0] + moment * (obstacle_speed * obstacles[2])
    centre_y = half_width * obstacles[1] + moment * (obstacle_speed * obstacles[3])
    reach = 1.25 + 0.75 * obstacles[4] + car_radius
    centre_x = jnp.take(centre_x, slot_row)[None, :, None, None]
    centre_y = jnp.take(centre_y, slot_row)[None, :, None, None]
    reach = jnp.take(reach, slot_row)[None, :, None, None]
    cosine = jnp.cos(angle_group)[:, None, None, None]
    sine = jnp.sin(angle_group)[:, None, None, None]
    nearest = None
    for offset in body_offsets:
        moved_x = x_cells[None, None, None, :] + offset * cosine
        moved_y = y_cells[None, None, :, None] + offset * sine
        clearance = (
            jnp.sqrt(jnp.square(moved_x - centre_x) + jnp.square(moved_y - centre_y)) - reach
        )
        closest = jnp.min(clearance, axis=1)
        nearest = closest if nearest is None else jnp.minimum(nearest, closest)
    return nearest


def clamp_edges(extended, margin):
    span_x = extended.shape[3]
    span_y = extended.shape[2]
    column_ids = lax.broadcasted_iota(jnp.int32, (1, 1, 1, span_x), 3)
    left_edge = jnp.logical_and(column_ids < margin, lax.axis_index("gx") == 0)
    right_edge = jnp.logical_and(
        column_ids >= span_x - margin, lax.axis_index("gx") == lax.axis_size("gx") - 1
    )
    extended = jnp.where(left_edge, extended[:, :, :, margin : margin + 1], extended)
    extended = jnp.where(
        right_edge, extended[:, :, :, span_x - margin - 1 : span_x - margin], extended
    )
    row_ids = lax.broadcasted_iota(jnp.int32, (1, 1, span_y, 1), 2)
    lower_edge = jnp.logical_and(row_ids < margin, lax.axis_index("gy") == 0)
    upper_edge = jnp.logical_and(
        row_ids >= span_y - margin, lax.axis_index("gy") == lax.axis_size("gy") - 1
    )
    extended = jnp.where(lower_edge, extended[:, :, margin : margin + 1, :], extended)
    extended = jnp.where(
        upper_edge, extended[:, :, span_y - margin - 1 : span_y - margin, :], extended
    )
    return extended


def heading_angles(offset_id, length, local_heads, total_heads):
    indices = (
        lax.axis_index("ha") * local_heads + offset_id + jnp.arange(length, dtype=jnp.int32)
    ) % total_heads
    return indices.astype(jnp.float32) * (2.0 * math.pi / total_heads) - math.pi


def local(value, obstacles, obstacle_slots, horizon, speed_offset):
    speed_count, local_heads, local_rows, local_cols = value.shape
    total_heads = local_heads * lax.axis_size("ha")
    step_x = 2.0 * half_width / (local_cols * lax.axis_size("gx"))
    step_y = 2.0 * half_width / (local_rows * lax.axis_size("gy"))
    step_h = 2.0 * math.pi / total_heads
    speeds = speed_step * (
        speed_offset.astype(jnp.float32)[0] + jnp.arange(speed_count, dtype=jnp.float32)
    )
    own_angles = heading_angles(0, local_heads, local_heads, total_heads)
    whole_angles = jnp.arange(total_heads, dtype=jnp.int32).astype(jnp.float32) * step_h - math.pi
    spread_x, spread_y, fastest = speed_bounds(speeds, whole_angles, step_x, step_y)
    rate_total = fastest + turn_limit / step_h + accel_limit / speed_step
    time_step = cfl_number / rate_total
    spacings = (speed_step, step_h, step_y, step_x)

    def advance_rims(surface):
        heading_ext = extended_2(surface, (("ha", 1),), 2, True)
        position_ext = extended_2(surface, (("gx", 3), ("gy", 2)), 2, False)
        position_ext = clamp_edges(position_ext, 2)
        pieces = (
            jnp.pad(surface, ((2, 2), (0, 0), (0, 0), (0, 0)), mode="edge"),
            heading_ext,
            position_ext[:, :, :, 2:-2],
            position_ext[:, :, 2:-2, :],
        )
        return surface + time_step * hamiltonian_rate(
            pieces, speeds, own_angles, (spread_x, spread_y), spacings
        )

    section_one = advance_rims(value)
    section_two = advance_rims(section_one)
    column_cells = (
        lax.axis_index("gx") * local_cols + jnp.arange(local_cols, dtype=jnp.int32)
    ).astype(jnp.float32)
    row_cells = (
        lax.axis_index("gy") * local_rows + jnp.arange(local_rows, dtype=jnp.int32)
    ).astype(jnp.float32)
    x_cells = (column_cells + 0.5) * step_x - half_width
    y_cells = (row_cells + 0.5) * step_y - half_width

    def one_group(packed):
        return group_field(obstacles, horizon, time_step, x_cells, y_cells, packed[0], packed[1])

    groups_local = local_heads // GH
    failure = lax.map(one_group, (own_angles.reshape(groups_local, GH), obstacle_slots))
    failure = failure.reshape(local_heads, local_rows, local_cols)
    return jnp.minimum(0.5 * (value + section_two), failure[None])


def solution(mesh):
    in_specs = (P(None, "ha", "gy", "gx"), P(), P("ha", None), P(), P())
    out_specs = P(None, "ha", "gy", "gx")
    return jax.shard_map(local, mesh=mesh, in_specs=in_specs, out_specs=out_specs, check_vma=False)
```

profile of v0, /device:TPU:1, one launch (start us, length us, event | category | flops | bytes accessed | tf_op | source)
XLA Modules:
  0.0 56.6 jit_solution(10297017778196113136)
XLA Ops:
  0.0 1.1 %fusion.85 = (f32[4,8,8,2]{3,2,1,0:T(8,128)S(1)}, f32[4,8,8,2]{3,2,1,0:T(8,128)S(1)}) fusion(f32[4,8,8,128]{3,2,1,0:T(8,128)} %param.9), kind=kLoop, calls=%fused_computation.218 | loop fusion | bytes 8192 | tf_op jit(solution)/shard_map/slice | solution.py:27
  1.2 4.5 %collective-permute-start = (f32[4,8,8,2]{3,2,1,0:T(8,128)S(1)}, f32[4,8,8,2]{3,2,1,0:T(8,128)S(1)}, u32[]{:S(2)}, u32[]{:S(2)}) collective-permute-start(f32[4,8,8,2]{3,2,1,0:T(8,128)S(1)} %get-tuple-element.227), channel_id=1, source_target_pairs={{0,8},{8,16},{16,24},{1,9},{9,17},{17,25},{2,10},{10,18},{18,26},{... | collective-permute-start | bytes 6152 | tf_op jit(solution)/shard_map/ppermute | solution.py:29
  5.7 1.9 %collective-permute-start.1 = (f32[4,8,8,2]{3,2,1,0:T(8,128)S(1)}, f32[4,8,8,2]{3,2,1,0:T(8,128)S(1)}, u32[]{:S(2)}, u32[]{:S(2)}) collective-permute-start(f32[4,8,8,2]{3,2,1,0:T(8,128)S(1)} %get-tuple-element.228), channel_id=1, source_target_pairs={{8,0},{16,8},{24,16},{9,1},{17,9},{25,17},{10,2},{18,10},{26,18},{... | collective-permute-start | bytes 6152 | tf_op jit(solution)/shard_map/ppermute | solution.py:30
  7.6 1.3 %collective-permute-start.4 = (f32[4,2,8,128]{3,2,1,0:T(8,128)S(1)}, f32[4,2,8,128]{3,2,1,0:T(8,128)S(1)}, u32[]{:S(2)}, u32[]{:S(2)}) collective-permute-start(f32[4,2,8,128]{3,2,1,0:T(8,128)S(1)} %get-tuple-element.231), channel_id=1, source_target_pairs={{0,1},{1,0},{2,3},{3,2},{4,5},{5,4},{6,7},{7,6},{8,9},{9,8},{10,11... | collective-permute-start | bytes 98312 | tf_op jit(solution)/shard_map/ppermute | solution.py:29
  8.9 0.3 collective-permute-start.5
  9.2 0.1 fusion.81
  10.7 0.7 %add_reduce_fusion = (f32[]{:T(128)}, f32[]{:T(128)}, f32[]{:T(128)}) fusion(f32[16]{0:T(128)S(1)} %get-tuple-element.237, f32[16]{0:T(128)S(1)} %get-tuple-element.238, f32[4]{0:T(128)S(1)} %add_multiply_fusion.6), kind=kLoop, calls=%fused_computation.191 | loop fusion | flops 637 | bytes 156 | tf_op jit(solution)/shard_map/reduce_max | solution.py:80
  12.0 0.0 copy-start.1
  12.0 0.0 copy-start.2
  12.0 0.6 %copy-done.1 = f32[5,128]{1,0:T(8,128)S(1)} copy-done((f32[5,128]{1,0:T(8,128)S(1)}, f32[5,128]{1,0:T(8,128)}, u32[]{:S(2)}) %copy-start.1) | copy-done | bytes 2584
  12.6 0.0 copy-done.2
  12.7 5.6 %while.14 = (s32[]{:T(128)}, f32[2,4,8,128]{3,2,1,0:T(8,128)S(1)}, f32[2,4]{1,0:T(2,128)S(1)}, f32[5,128]{1,0:T(8,128)S(1)}, f32[]{:T(128)}, /*index=5*/s32[2,16]{1,0:T(2,128)S(1)}, s32[]{:T(128)}, s32[]{:T(128)}, s32[]{:T(128)}) while((s32[]{:T(128)}, f32[2,4,8,128]{3,2,1,0:T(8,128)S(1)}, f32[2,4]{1,0:T(2,128)S(1)}, ...), condition=%wide.region_7.9_spmd.clone, body=%wide.region_3.8_spmd.clone.sunk | while | flops 642522 | bytes 347689 | solution.py:181
  12.7 0.7 %gather_fusion.1 = f32[16]{0:T(128)S(1)} fusion(f32[128]{0:T(128)S(1)} %get-tuple-element.318, s32[1024]{0:T(1024)S(1)} %pad_clamp_fusion.2), kind=kCustom, calls=%fused_computation.1.clone.clone.1 | custom fusion | bytes 192 | tf_op jit(solution)/shard_map/while/body/eval_jaxpr/jit(_take)/gather | solution.py:89
  13.4 0.7 %gather_fusion.2 = f32[16]{0:T(128)S(1)} fusion(f32[128]{0:T(128)S(1)} %get-tuple-element.319, s32[1024]{0:T(1024)S(1)} %pad_clamp_fusion.2), kind=kCustom, calls=%fused_computation.clone.clone.1 | custom fusion | bytes 192 | tf_op jit(solution)/shard_map/while/body/eval_jaxpr/jit(_take)/gather | solution.py:88
  14.0 0.7 %gather_fusion = f32[16]{0:T(128)S(1)} fusion(f32[128]{0:T(128)S(1)} %get-tuple-element.317, s32[1024]{0:T(1024)S(1)} %pad_clamp_fusion.2), kind=kCustom, calls=%fused_computation.2.clone.clone.1 | custom fusion | bytes 192 | tf_op jit(solution)/shard_map/while/body/eval_jaxpr/jit(_take)/gather | solution.py:90
  14.8 0.1 broadcast_add_fusion.9
  14.9 0.1 subtract_multiply_fusion.13
  15.0 0.1 broadcast_add_fusion.8
  15.1 0.1 subtract_multiply_fusion.12
  15.2 0.3 subtract_reduce_fusion.4
  15.6 0.7 %gather_fusion.1 = f32[16]{0:T(128)S(1)} fusion(f32[128]{0:T(128)S(1)} %get-tuple-element.318, s32[1024]{0:T(1024)S(1)} %pad_clamp_fusion.2), kind=kCustom, calls=%fused_computation.1.clone.clone.1 | custom fusion | bytes 192 | tf_op jit(solution)/shard_map/while/body/eval_jaxpr/jit(_take)/gather | solution.py:89
  16.2 0.7 %gather_fusion.2 = f32[16]{0:T(128)S(1)} fusion(f32[128]{0:T(128)S(1)} %get-tuple-element.319, s32[1024]{0:T(1024)S(1)} %pad_clamp_fusion.2), kind=kCustom, calls=%fused_computation.clone.clone.1 | custom fusion | bytes 192 | tf_op jit(solution)/shard_map/while/body/eval_jaxpr/jit(_take)/gather | solution.py:88
  16.9 0.7 %gather_fusion = f32[16]{0:T(128)S(1)} fusion(f32[128]{0:T(128)S(1)} %get-tuple-element.317, s32[1024]{0:T(1024)S(1)} %pad_clamp_fusion.2), kind=kCustom, calls=%fused_computation.2.clone.clone.1 | custom fusion | bytes 192 | tf_op jit(solution)/shard_map/while/body/eval_jaxpr/jit(_take)/gather | solution.py:90
  17.7 0.1 broadcast_add_fusion.9
  17.7 0.1 subtract_multiply_fusion.13
  17.8 0.1 broadcast_add_fusion.8
  17.9 0.1 subtract_multiply_fusion.12
  18.0 0.3 subtract_reduce_fusion.4
  18.3 0.1 multiply_multiply_fusion.1
  18.4 0.0 collective-permute-done
  18.4 0.3 pad_maximum_fusion.13
  18.7 3.2 %collective-permute-start.2 = (f32[4,8,2,132]{3,1,2,0:T(8,128)S(1)}, f32[4,8,2,132]{3,1,2,0:T(8,128)S(1)}, u32[]{:S(2)}, u32[]{:S(2)}) collective-permute-start(f32[4,8,2,132]{3,1,2,0:T(8,128)S(1)} %copy.169), channel_id=1, source_target_pairs={{0,2},{2,4},{4,6},{1,3},{3,5},{5,7},{8,10},{10,12},{12,14},{9,11},... | collective-permute-start | bytes 101384 | tf_op jit(solution)/shard_map/ppermute | solution.py:29
  22.0 1.3 %collective-permute-start.3 = (f32[4,8,2,132]{3,1,2,0:T(8,128)S(1)}, f32[4,8,2,132]{3,1,2,0:T(8,128)S(1)}, u32[]{:S(2)}, u32[]{:S(2)}) collective-permute-start(f32[4,8,2,132]{3,1,2,0:T(8,128)S(1)} %copy.170), channel_id=1, source_target_pairs={{2,0},{4,2},{6,4},{3,1},{5,3},{7,5},{10,8},{12,10},{14,12},{11,9},... | collective-permute-start | bytes 101384 | tf_op jit(solution)/shard_map/ppermute | solution.py:30
  23.3 0.0 collective-permute-done.4
  23.3 0.0 collective-permute-done.5
  23.4 3.7 %collective-permute-done.3 = f32[4,8,2,132]{3,1,2,0:T(8,128)S(1)} collective-permute-done((f32[4,8,2,132]{3,1,2,0:T(8,128)S(1)}, f32[4,8,2,132]{3,1,2,0:T(8,128)S(1)}, u32[]{:S(2)}, u32[]{:S(2)}) %collective-permute-start.3) | collective-permute-done | bytes 33824 | tf_op jit(solution)/shard_map/ppermute | solution.py:30
  27.1 0.3 pad_maximum_fusion
  27.4 0.3 slice_reduce_fusion.3
  27.6 0.3 broadcast_select_fusion.10
  28.0 0.3 slice_reduce_fusion.2
  28.3 0.1 broadcast_select_fusion.9
  28.5 0.1 broadcast_select_fusion.8
  28.7 0.2 broadcast_select_fusion.7
  28.9 2.5 %multiply_add_fusion.2 = f32[4,8,8,128]{3,2,1,0:T(8,128)S(1)} fusion(f32[4,8,8,128]{3,2,1,0:T(8,128)S(1)} %copy-done, f32[2,8,8,128]{3,2,1,0:T(8,128)S(1)} %reshape.478, f32[2,8,8,128]{3,2,1,0:T(8,128)S(1)} %reshape.477, f32[4,10,8,128]{3,2,1,0:T(8,128)S(1)} %constant_dynamic-update-slice_fusion.2, f32[4,10,8,128]{3,2,1,0:T(8,128)S(1)} %get-tuple-element.229, ...), kind=kLoop, calls=%fused_computation.134 | loop fusion | flops 7012352 | bytes 2097420 | tf_op jit(solution)/shard_map/add | solution.py:162
  31.3 0.1 fusion.83
  31.4 5.5 %collective-permute-start.6 = (f32[4,8,8,2]{3,2,1,0:T(8,128)S(1)}, f32[4,8,8,2]{3,2,1,0:T(8,128)S(1)}, u32[]{:S(2)}, u32[]{:S(2)}) collective-permute-start(f32[4,8,8,2]{3,2,1,0:T(8,128)S(1)} %get-tuple-element.221), channel_id=1, source_target_pairs={{0,8},{8,16},{16,24},{1,9},{9,17},{17,25},{2,10},{10,18},{18,26},{... | collective-permute-start | bytes 6152 | tf_op jit(solution)/shard_map/ppermute | solution.py:29
  37.0 1.9 %collective-permute-start.7 = (f32[4,8,8,2]{3,2,1,0:T(8,128)S(1)}, f32[4,8,8,2]{3,2,1,0:T(8,128)S(1)}, u32[]{:S(2)}, u32[]{:S(2)}) collective-permute-start(f32[4,8,8,2]{3,2,1,0:T(8,128)S(1)} %get-tuple-element.222), channel_id=1, source_target_pairs={{8,0},{16,8},{24,16},{9,1},{17,9},{25,17},{10,2},{18,10},{26,18},{... | collective-permute-start | bytes 6152 | tf_op jit(solution)/shard_map/ppermute | solution.py:30
  38.9 4.3 %collective-permute-done.7 = f32[4,8,8,2]{3,2,1,0:T(8,128)S(1)} collective-permute-done((f32[4,8,8,2]{3,2,1,0:T(8,128)S(1)}, f32[4,8,8,2]{3,2,1,0:T(8,128)S(1)}, u32[]{:S(2)}, u32[]{:S(2)}) %collective-permute-start.7) | collective-permute-done | bytes 2080 | tf_op jit(solution)/shard_map/ppermute | solution.py:30
  43.3 0.3 pad_maximum_fusion.10
  43.5 3.2 %collective-permute-start.8 = (f32[4,8,2,132]{3,1,2,0:T(8,128)S(1)}, f32[4,8,2,132]{3,1,2,0:T(8,128)S(1)}, u32[]{:S(2)}, u32[]{:S(2)}) collective-permute-start(f32[4,8,2,132]{3,1,2,0:T(8,128)S(1)} %copy.161), channel_id=1, source_target_pairs={{0,2},{2,4},{4,6},{1,3},{3,5},{5,7},{8,10},{10,12},{12,14},{9,11},... | collective-permute-start | bytes 101384 | tf_op jit(solution)/shard_map/ppermute | solution.py:29
  46.8 1.3 %collective-permute-start.9 = (f32[4,8,2,132]{3,1,2,0:T(8,128)S(1)}, f32[4,8,2,132]{3,1,2,0:T(8,128)S(1)}, u32[]{:S(2)}, u32[]{:S(2)}) collective-permute-start(f32[4,8,2,132]{3,1,2,0:T(8,128)S(1)} %copy.162), channel_id=1, source_target_pairs={{2,0},{4,2},{6,4},{3,1},{5,3},{7,5},{10,8},{12,10},{14,12},{11,9},... | collective-permute-start | bytes 101384 | tf_op jit(solution)/shard_map/ppermute | solution.py:30
  48.1 1.3 %collective-permute-start.10 = (f32[4,2,8,128]{3,2,1,0:T(8,128)S(1)}, f32[4,2,8,128]{3,2,1,0:T(8,128)S(1)}, u32[]{:S(2)}, u32[]{:S(2)}) collective-permute-start(f32[4,2,8,128]{3,2,1,0:T(8,128)S(1)} %get-tuple-element.223), channel_id=1, source_target_pairs={{0,1},{1,0},{2,3},{3,2},{4,5},{5,4},{6,7},{7,6},{8,9},{9,8},{10,11... | collective-permute-start | bytes 98312 | tf_op jit(solution)/shard_map/ppermute | solution.py:29
  49.4 0.3 collective-permute-start.11
  49.6 0.0 collective-permute-done.8
  49.7 2.1 %collective-permute-done.9 = f32[4,8,2,132]{3,1,2,0:T(8,128)S(1)} collective-permute-done((f32[4,8,2,132]{3,1,2,0:T(8,128)S(1)}, f32[4,8,2,132]{3,1,2,0:T(8,128)S(1)}, u32[]{:S(2)}, u32[]{:S(2)}) %collective-permute-start.9) | collective-permute-done | bytes 33824 | tf_op jit(solution)/shard_map/ppermute | solution.py:30
  51.8 0.3 pad_maximum_fusion.1
  52.1 0.3 slice_reduce_fusion.1
  52.4 0.3 broadcast_select_fusion.6
  52.7 0.3 slice_reduce_fusion
  53.0 0.1 broadcast_select_fusion.5
  53.2 0.1 broadcast_select_fusion.4
  53.4 0.2 broadcast_select_fusion.3
  53.6 0.0 collective-permute-done.10
  53.6 3.0 %multiply_minimum_fusion = f32[4,8,8,128]{3,2,1,0:T(8,128)} fusion(f32[4,8,8,128]{3,2,1,0:T(8,128)S(1)} %copy-done, f32[4,8,8,128]{3,2,1,0:T(8,128)S(1)} %multiply_add_fusion.2, f32[2,8,8,128]{3,2,1,0:T(8,128)S(1)} %reshape.480, f32[2,8,8,128]{3,2,1,0:T(8,128)S(1)} %reshape.479, f32[4,2,8,128]{3,2,1,0:T(8,128)S(1)} %collective-permute-done.11, ...), kind=kLoop, calls=%fused_computation.101 | loop fusion | flops 7241728 | bytes 1802508 | tf_op jit(solution)/shard_map/min | solution.py:183
  (59 shorter events, 0.8 us)
Async XLA Ops:
  0.0 7.6 %copy-start = (f32[4,8,8,128]{3,2,1,0:T(8,128)S(1)}, f32[4,8,8,128]{3,2,1,0:T(8,128)}, u32[]{:S(2)}) copy-start(f32[4,8,8,128]{3,2,1,0:T(8,128)} %param.9) | copy-start | bytes 393220
  1.2 17.3 %collective-permute-start = (f32[4,8,8,2]{3,2,1,0:T(8,128)S(1)}, f32[4,8,8,2]{3,2,1,0:T(8,128)S(1)}, u32[]{:S(2)}, u32[]{:S(2)}) collective-permute-start(f32[4,8,8,2]{3,2,1,0:T(8,128)S(1)} %get-tuple-element.227), channel_id=1, source_target_pairs={{0,8},{8,16},{16,24},{1,9},{9,17},{17,25},{2,10},{10,18},{18,26},{... | collective-permute-start | bytes 6152 | tf_op jit(solution)/shard_map/ppermute | solution.py:29
  5.7 12.8 %collective-permute-start.1 = (f32[4,8,8,2]{3,2,1,0:T(8,128)S(1)}, f32[4,8,8,2]{3,2,1,0:T(8,128)S(1)}, u32[]{:S(2)}, u32[]{:S(2)}) collective-permute-start(f32[4,8,8,2]{3,2,1,0:T(8,128)S(1)} %get-tuple-element.228), channel_id=1, source_target_pairs={{8,0},{16,8},{24,16},{9,1},{17,9},{25,17},{10,2},{18,10},{26,18},{... | collective-permute-start | bytes 6152 | tf_op jit(solution)/shard_map/ppermute | solution.py:30
  7.6 15.6 %collective-permute-start.4 = (f32[4,2,8,128]{3,2,1,0:T(8,128)S(1)}, f32[4,2,8,128]{3,2,1,0:T(8,128)S(1)}, u32[]{:S(2)}, u32[]{:S(2)}) collective-permute-start(f32[4,2,8,128]{3,2,1,0:T(8,128)S(1)} %get-tuple-element.231), channel_id=1, source_target_pairs={{0,1},{1,0},{2,3},{3,2},{4,5},{5,4},{6,7},{7,6},{8,9},{9,8},{10,11... | collective-permute-start | bytes 98312 | tf_op jit(solution)/shard_map/ppermute | solution.py:29
  8.9 14.4 %collective-permute-start.5 = (f32[4,2,8,128]{3,2,1,0:T(8,128)S(1)}, f32[4,2,8,128]{3,2,1,0:T(8,128)S(1)}, u32[]{:S(2)}, u32[]{:S(2)}) collective-permute-start(f32[4,2,8,128]{3,2,1,0:T(8,128)S(1)} %get-tuple-element.232), channel_id=1, source_target_pairs={{1,0},{0,1},{3,2},{2,3},{5,4},{4,5},{7,6},{6,7},{9,8},{8,9},{11,10... | collective-permute-start | bytes 98312 | tf_op jit(solution)/shard_map/ppermute | solution.py:30
  12.0 0.7 %copy-start.1 = (f32[5,128]{1,0:T(8,128)S(1)}, f32[5,128]{1,0:T(8,128)}, u32[]{:S(2)}) copy-start(f32[5,128]{1,0:T(8,128)} %param.10) | copy-start | bytes 7684
  12.0 0.7 %copy-start.2 = (s32[2,16]{1,0:T(2,128)S(1)}, s32[2,16]{1,0:T(2,128)}, u32[]{:S(2)}) copy-start(s32[2,16]{1,0:T(2,128)} %param.11) | copy-start | bytes 388
  18.7 4.6 %collective-permute-start.2 = (f32[4,8,2,132]{3,1,2,0:T(8,128)S(1)}, f32[4,8,2,132]{3,1,2,0:T(8,128)S(1)}, u32[]{:S(2)}, u32[]{:S(2)}) collective-permute-start(f32[4,8,2,132]{3,1,2,0:T(8,128)S(1)} %copy.169), channel_id=1, source_target_pairs={{0,2},{2,4},{4,6},{1,3},{3,5},{5,7},{8,10},{10,12},{12,14},{9,11},... | collective-permute-start | bytes 101384 | tf_op jit(solution)/shard_map/ppermute | solution.py:29
  22.0 5.1 %collective-permute-start.3 = (f32[4,8,2,132]{3,1,2,0:T(8,128)S(1)}, f32[4,8,2,132]{3,1,2,0:T(8,128)S(1)}, u32[]{:S(2)}, u32[]{:S(2)}) collective-permute-start(f32[4,8,2,132]{3,1,2,0:T(8,128)S(1)} %copy.170), channel_id=1, source_target_pairs={{2,0},{4,2},{6,4},{3,1},{5,3},{7,5},{10,8},{12,10},{14,12},{11,9},... | collective-permute-start | bytes 101384 | tf_op jit(solution)/shard_map/ppermute | solution.py:30
  31.4 7.5 %collective-permute-start.6 = (f32[4,8,8,2]{3,2,1,0:T(8,128)S(1)}, f32[4,8,8,2]{3,2,1,0:T(8,128)S(1)}, u32[]{:S(2)}, u32[]{:S(2)}) collective-permute-start(f32[4,8,8,2]{3,2,1,0:T(8,128)S(1)} %get-tuple-element.221), channel_id=1, source_target_pairs={{0,8},{8,16},{16,24},{1,9},{9,17},{17,25},{2,10},{10,18},{18,26},{... | collective-permute-start | bytes 6152 | tf_op jit(solution)/shard_map/ppermute | solution.py:29
  37.0 6.3 %collective-permute-start.7 = (f32[4,8,8,2]{3,2,1,0:T(8,128)S(1)}, f32[4,8,8,2]{3,2,1,0:T(8,128)S(1)}, u32[]{:S(2)}, u32[]{:S(2)}) collective-permute-start(f32[4,8,8,2]{3,2,1,0:T(8,128)S(1)} %get-tuple-element.222), channel_id=1, source_target_pairs={{8,0},{16,8},{24,16},{9,1},{17,9},{25,17},{10,2},{18,10},{26,18},{... | collective-permute-start | bytes 6152 | tf_op jit(solution)/shard_map/ppermute | solution.py:30
  43.5 6.1 %collective-permute-start.8 = (f32[4,8,2,132]{3,1,2,0:T(8,128)S(1)}, f32[4,8,2,132]{3,1,2,0:T(8,128)S(1)}, u32[]{:S(2)}, u32[]{:S(2)}) collective-permute-start(f32[4,8,2,132]{3,1,2,0:T(8,128)S(1)} %copy.161), channel_id=1, source_target_pairs={{0,2},{2,4},{4,6},{1,3},{3,5},{5,7},{8,10},{10,12},{12,14},{9,11},... | collective-permute-start | bytes 101384 | tf_op jit(solution)/shard_map/ppermute | solution.py:29
  46.8 5.0 %collective-permute-start.9 = (f32[4,8,2,132]{3,1,2,0:T(8,128)S(1)}, f32[4,8,2,132]{3,1,2,0:T(8,128)S(1)}, u32[]{:S(2)}, u32[]{:S(2)}) collective-permute-start(f32[4,8,2,132]{3,1,2,0:T(8,128)S(1)} %copy.162), channel_id=1, source_target_pairs={{2,0},{4,2},{6,4},{3,1},{5,3},{7,5},{10,8},{12,10},{14,12},{11,9},... | collective-permute-start | bytes 101384 | tf_op jit(solution)/shard_map/ppermute | solution.py:30
  48.1 5.5 %collective-permute-start.10 = (f32[4,2,8,128]{3,2,1,0:T(8,128)S(1)}, f32[4,2,8,128]{3,2,1,0:T(8,128)S(1)}, u32[]{:S(2)}, u32[]{:S(2)}) collective-permute-start(f32[4,2,8,128]{3,2,1,0:T(8,128)S(1)} %get-tuple-element.223), channel_id=1, source_target_pairs={{0,1},{1,0},{2,3},{3,2},{4,5},{5,4},{6,7},{7,6},{8,9},{9,8},{10,11... | collective-permute-start | bytes 98312 | tf_op jit(solution)/shard_map/ppermute | solution.py:29
  49.4 4.2 %collective-permute-start.11 = (f32[4,2,8,128]{3,2,1,0:T(8,128)S(1)}, f32[4,2,8,128]{3,2,1,0:T(8,128)S(1)}, u32[]{:S(2)}, u32[]{:S(2)}) collective-permute-start(f32[4,2,8,128]{3,2,1,0:T(8,128)S(1)} %get-tuple-element.224), channel_id=1, source_target_pairs={{1,0},{0,1},{3,2},{2,3},{5,4},{4,5},{7,6},{6,7},{9,8},{8,9},{11,10... | collective-permute-start | bytes 98312 | tf_op jit(solution)/shard_map/ppermute | solution.py:30
where the time goes:
time: 57.1 us; the launch traced here: 56.6 us
  starting transfers between devices  26 us (46%)
  other arithmetic  10.7 us (19%)
  waiting for transfers between devices  10.1 us (18%)
  local copies, waits for them, and re-layouts  7.31 us (13%)
  between operations  2.43 us (4%)
    ppermute x6, starting transfers between devices, extended_2(): before = lax.ppermute(last, axis, up)  19 us
    ppermute x6, waiting for transfers between devices, extended_2(): after = lax.ppermute(initial, axis, down)  10.1 us
    ppermute x6, starting transfers between devices, extended_2(): after = lax.ppermute(initial, axis, down)  6.93 us
    min x1, other arithmetic, local(): return jnp.minimum(0.5 * (value + section_two), failure[None])  3.05 us
    add x1, other arithmetic, advance_rims(): surface + time_step * hamiltonian_rate(pieces, speeds, own_angles, (sprea...  2.45 us
    gather x2, local copies, waits for them, and re-layouts, group_field(): centre_x = jnp.take(centre_x, slot_row)[None, :, None, None]  1.33 us
    gather x2, local copies, waits for them, and re-layouts, group_field(): reach = jnp.take(reach, slot_row)[None, :, None, None]  1.33 us
    gather x2, local copies, waits for them, and re-layouts, group_field(): centre_y = jnp.take(centre_y, slot_row)[None, :, None, None]  1.31 us
  transfers between devices with their start and end apart: 12, of which 3 were waited for; matrix products, arithmetic and copies ran while one was open for 15% of the time, Pallas kernels for 0%

commit v1 on v0

v1 whole, which is shorter than its diff:
```python
import functools
import math

import jax
import jax.numpy as jnp
import numpy as np
from jax import lax
from jax.experimental import pallas as pl
from jax.experimental.pallas import tpu as pltpu
from jax.sharding import PartitionSpec as P

GH = 4

cfl_number = 0.75
weno_eps = 1e-06
half_width = 20.0
speed_step = 0.5
turn_limit = 1.0
accel_limit = 4.0
obstacle_speed = 2.0
car_radius = 0.8

DEPTH = 4
SLOT = 2 * DEPTH


class Plan:
    def __init__(self, mesh, shape):
        self.speeds, self.heads, self.rows, self.cols = shape
        self.axes = dict(mesh.shape)
        self.total_heads = self.heads * self.axes["ha"]
        self.step_x = 2.0 * half_width / (self.cols * self.axes["gx"])
        self.step_y = 2.0 * half_width / (self.rows * self.axes["gy"])
        self.step_h = 2.0 * math.pi / self.total_heads
        assert self.rows == 2 * DEPTH and self.heads >= DEPTH and self.heads % GH == 0
        assert SLOT * (self.heads + DEPTH) <= self.cols
        assert all(size % 2 == 0 for size in self.axes.values())
        index = np.arange(self.total_heads, dtype=np.float32)
        angles = index * np.float32(self.step_h) - np.float32(math.pi)
        self.cosines = np.cos(angles.astype(np.float64))
        self.sines = np.sin(angles.astype(np.float64))
        self.most_cos = float(np.max(np.abs(self.cosines)))
        self.most_sin = float(np.max(np.abs(self.sines)))
        self.most_rate = float(
            np.max(np.abs(self.cosines) / self.step_x + np.abs(self.sines) / self.step_y)
        )

    def trig(self, head):
        place = lax.axis_index("ha")
        picked = []
        for table in (self.cosines, self.sines):
            values = [
                float(table[(a * self.heads + head) % self.total_heads])
                for a in range(self.axes["ha"])
            ]
            value = jnp.float32(values[0])
            for a in range(1, len(values)):
                value = jnp.where(place == a, jnp.float32(values[a]), value)
            picked.append(value)
        return picked

    def pace(self, offset_ref):
        base = offset_ref[0].astype(jnp.float32)
        speeds = [speed_step * (base + float(k)) for k in range(self.speeds)]
        top = functools.reduce(jnp.maximum, [jnp.abs(speed) for speed in speeds])
        total = top * self.most_rate + (turn_limit / self.step_h + accel_limit / speed_step)
        time_step = cfl_number / jnp.full((self.rows, self.cols), total, jnp.float32)
        return speeds, (top * self.most_cos, top * self.most_sin), time_step


def partners(axis, odd, wrap):
    count = lax.axis_size(axis)
    pairs = []
    for i in range(1 if odd else 0, count, 2):
        j = i + 1
        if j < count or wrap:
            pairs += [(i, j % count), (j % count, i)]
    return pairs


def swap(payload, axis, odd, wrap=False):
    return lax.ppermute(payload, axis, partners(axis, odd, wrap))


def by_side(axis, even_block, odd_block):
    is_even = lax.axis_index(axis) % 2 == 0
    return jnp.where(is_even, odd_block, even_block), jnp.where(is_even, even_block, odd_block)


def is_first(axis):
    return lax.axis_index(axis) == 0


def is_last(axis):
    return lax.axis_index(axis) == lax.axis_size(axis) - 1


def call(body, plan, out_shapes, args, specs, scratch=(), flops=1000000):
    space = {"v": pltpu.VMEM, "s": pltpu.SMEM}
    return pl.pallas_call(
        functools.partial(body, plan),
        out_shape=[jax.ShapeDtypeStruct(shape, jnp.float32) for shape in out_shapes],
        in_specs=[pl.BlockSpec(memory_space=space[s]) for s in specs],
        out_specs=[pl.BlockSpec(memory_space=pltpu.VMEM) for _ in out_shapes],
        scratch_shapes=scratch,
        name=body.__name__,
        cost_estimate=pl.CostEstimate(flops=flops, bytes_accessed=400000, transcendentals=0),
    )(*args)


def iota(plan, dim):
    return lax.broadcasted_iota(jnp.int32, (plan.rows, plan.cols), dim)


def pack_rows(plan, value, even_out, odd_out):
    row = iota(plan, 0)
    is_even = lax.axis_index("gy") % 2 == 0
    for v in range(plan.speeds):
        for pair in range(plan.heads // 2):
            one, two = value[v, 2 * pair], value[v, 2 * pair + 1]
            low = jnp.where(row < DEPTH, one, pltpu.roll(two, DEPTH, 0))
            high = jnp.where(row < DEPTH, pltpu.roll(one, DEPTH, 0), two)
            even_out[v, pair] = jnp.where(is_even, high, low)
            odd_out[v, pair] = jnp.where(is_even, low, high)


def unpack_rows(plan, value, even_in, odd_in, ring_out, corner_out):
    row = iota(plan, 0)
    at_first = jnp.logical_and(row >= DEPTH, is_first("gy"))
    at_last = jnp.logical_and(row < DEPTH, is_last("gy"))
    inner = jnp.logical_or(row < 2, row >= plan.rows - 2)
    edge_heads = (0, 1, plan.heads - 2, plan.heads - 1)
    for v in range(plan.speeds):
        kept = {}
        for pair in range(plan.heads // 2):
            before, after = by_side("gy", even_in[v, pair], odd_in[v, pair])
            one = jnp.where(row < DEPTH, after, pltpu.roll(before, DEPTH, 0))
            two = jnp.where(row < DEPTH, pltpu.roll(after, DEPTH, 0), before)
            for h, ring in ((2 * pair, one), (2 * pair + 1, two)):
                ring = clamp_rows(plan, value[v, h], ring, at_first, at_last)
                ring_out[v, h] = ring
                kept[h] = ring
        for side in range(2):
            one, two = kept[edge_heads[2 * side]], kept[edge_heads[2 * side + 1]]
            corner_out[v, side] = jnp.where(inner, one, pltpu.roll(two, DEPTH, 0))


def clamp_rows(plan, own, ring, at_first, at_last):
    shape = (plan.rows, plan.cols)
    ring = jnp.where(at_first, jnp.broadcast_to(own[0:1], shape), ring)
    return jnp.where(at_last, jnp.broadcast_to(own[plan.rows - 1 :], shape), ring)


def clamp_cols(plan, own, ring, at_first, at_last):
    shape = (plan.rows, plan.cols)
    ring = jnp.where(at_first, jnp.broadcast_to(own[:, 0:1], shape), ring)
    return jnp.where(at_last, jnp.broadcast_to(own[:, plan.cols - 1 :], shape), ring)


def pack_cols(plan, value, heads_even, heads_odd, ring, packed_out):
    slot_id = iota(plan, 1) // SLOT
    for v in range(plan.speeds):
        packed = jnp.zeros((plan.rows, plan.cols), jnp.float32)
        for h in range(-2, plan.heads + 2):
            block = head_block(plan, value, heads_even, heads_odd, v, h)
            slot = h + 2
            packed = jnp.where(slot_id == slot, pltpu.roll(block, DEPTH + SLOT * slot, 1), packed)
        packed_out[v, 0] = packed
        packed = jnp.zeros((plan.rows, plan.cols), jnp.float32)
        for h in range(plan.heads):
            slot = h + 2
            moved = pltpu.roll(ring[v, h], DEPTH + SLOT * slot, 1)
            packed = jnp.where(slot_id == slot, moved, packed)
        packed_out[v, 1] = packed


def head_block(plan, value, heads_even, heads_odd, v, h):
    if 0 <= h < plan.heads:
        return value[v, h]
    source = h % plan.heads
    if heads_odd is None:
        return heads_even[v, source]
    sides = by_side("ha", heads_even[v, source], heads_odd[v, source])
    return sides[0] if h < 0 else sides[1]


def failure_field(plan, obstacles, slots, horizon, offset, failure_out):
    _, _, time_step = plan.pace(offset)
    moment = horizon[0] + time_step
    col = (lax.axis_index("gx") * plan.cols + iota(plan, 1)).astype(jnp.float32)
    row = (lax.axis_index("gy") * plan.rows + iota(plan, 0)).astype(jnp.float32)
    x_cells = (col + 0.5) * plan.step_x - half_width
    y_cells = (row + 0.5) * plan.step_y - half_width
    for group in range(plan.heads // GH):
        angles = [plan.trig(group * GH + g) for g in range(GH)]

        def step(slot, nearest):
            which = slots[group, slot]
            centre_x = half_width * obstacles[0, which]
            centre_y = half_width * obstacles[1, which]
            away_x = x_cells - (centre_x + moment * (obstacle_speed * obstacles[2, which]))
            away_y = y_cells - (centre_y + moment * (obstacle_speed * obstacles[3, which]))
            reach = 1.25 + 0.75 * obstacles[4, which] + car_radius
            middle = away_x * away_x + away_y * away_y
            updated = []
            for g in range(GH):
                cosine, sine = angles[g]
                front_x, front_y = away_x + cosine, away_y + sine
                back_x, back_y = away_x - cosine, away_y - sine
                squared = jnp.minimum(
                    middle,
                    jnp.minimum(
                        front_x * front_x + front_y * front_y, back_x * back_x + back_y * back_y
                    ),
                )
                updated.append(jnp.minimum(nearest[g], jnp.sqrt(squared) - reach))
            return tuple(updated)

        far = jnp.full((plan.rows, plan.cols), 1e30, jnp.float32)
        nearest = lax.fori_loop(0, slots.shape[1], step, (far,) * GH, unroll=2)
        for g in range(GH):
            failure_out[group * GH + g] = nearest[g]


def sharp(bend, floor):
    t = bend * bend + floor
    return t * t


def sides_of(bends, floor):
    before, here, after = bends
    half = 0.5 * sharp(here, floor)
    low = half + sharp(before, floor)
    high = half + sharp(after, floor)
    return (before - here) * high, (after - here) * low, half / (low * high)


def bends_of(samples):
    steps = [samples[i + 1] - samples[i] for i in range(4)]
    return [steps[i + 1] - steps[i] for i in range(3)], samples[3] - samples[1]


def drift_term(samples, floor, drift, spread, spacing):
    bends, across = bends_of(samples)
    a, b, r = sides_of(bends, floor)
    quarter = 0.25 / spacing
    return (drift * (0.5 / spacing)) * across + r * (
        ((spread + drift) * quarter) * a + ((spread - drift) * quarter) * b
    )


def limit_term(bends, across, floor, limit, spacing):
    a, b, r = sides_of(bends, floor)
    r = r * (0.25 * limit / spacing)
    return jnp.abs((0.5 * limit / spacing) * across + r * (a - b)) + r * (a + b)


def ring_samples(block, ring, place, axis, length):
    return [
        pltpu.roll(jnp.where(place >= length - 2, ring, block), 2, axis),
        pltpu.roll(jnp.where(place >= length - 1, ring, block), 1, axis),
        block,
        pltpu.roll(jnp.where(place < 1, ring, block), length - 1, axis),
        pltpu.roll(jnp.where(place < 2, ring, block), length - 2, axis),
    ]


def speed_terms(plan, blocks):
    floor = weno_eps * speed_step * speed_step
    count = len(blocks)
    at = lambda k: blocks[min(max(k, 0), count - 1)]
    steps = {k: at(k + 1) - at(k) for k in range(0, count - 1)}
    zero = jnp.zeros_like(blocks[0])
    step = lambda k: steps.get(k, zero)
    terms = []
    for k in range(count):
        bends = [step(k + j) - step(k + j - 1) for j in (-1, 0, 1)]
        terms.append(limit_term(bends, at(k + 1) - at(k - 1), floor, accel_limit, speed_step))
    return terms


def advanced(plan, blocks, row_samples, col_samples, head_samples, pace, trig):
    speeds, spreads, time_step = pace
    terms = speed_terms(plan, blocks)
    results = []
    for v, block in enumerate(blocks):
        bends, across = bends_of(head_samples[v])
        rate = terms[v] + limit_term(
            bends, across, weno_eps * plan.step_h**2, turn_limit, plan.step_h
        )
        rate = rate + drift_term(
            row_samples[v], weno_eps * plan.step_y**2, speeds[v] * trig[1], spreads[1], plan.step_y
        )
        rate = rate + drift_term(
            col_samples[v], weno_eps * plan.step_x**2, speeds[v] * trig[0], spreads[0], plan.step_x
        )
        results.append(block + time_step * jnp.minimum(rate, 0.0))
    return results


def step_kernel(plan, *refs):
    wide = plan.axes["ha"] > 2
    names = ["value", "heads_even"] + (["heads_odd"] if wide else [])
    names += ["ring", "corner_even"] + (["corner_odd"] if wide else [])
    names += ["packed", "cols_even", "cols_odd", "failure", "offset", "out"]
    names += ["f_a", "f_b", "x_a", "x_b", "s_a", "s_b", "x_s", "trig"]
    r = dict(zip(names, refs, strict=True))
    nv, heads, rows, cols = plan.speeds, plan.heads, plan.rows, plan.cols
    heads_odd, corner_odd = r.get("heads_odd"), r.get("corner_odd")
    pace = plan.pace(r["offset"])
    row, col = iota(plan, 0), iota(plan, 1)
    lower = col % SLOT < DEPTH
    row_first = jnp.logical_and(row >= DEPTH, is_first("gy"))
    row_last = jnp.logical_and(row < DEPTH, is_last("gy"))
    col_first = jnp.logical_and(col >= cols // 2, is_first("gx"))
    col_last = jnp.logical_and(col < cols // 2, is_last("gx"))
    f_a, f_b, x_a, x_b = r["f_a"], r["f_b"], r["x_a"], r["x_b"]
    s_a, s_b, x_s = r["s_a"], r["s_b"], r["x_s"]

    cos_lanes = jnp.zeros((rows, cols), jnp.float32)
    sin_lanes = jnp.zeros((rows, cols), jnp.float32)
    for h in range(-2, heads + 2):
        cosine, sine = plan.trig(h)
        r["trig"][0, h + 2] = cosine
        r["trig"][1, h + 2] = sine
        cos_lanes = jnp.where(col // SLOT == h + 2, cosine, cos_lanes)
        sin_lanes = jnp.where(col // SLOT == h + 2, sine, sin_lanes)

    around = []
    for v in range(nv):
        for h in range(-DEPTH, heads + DEPTH):
            f_a[v, h + DEPTH] = head_block(plan, r["value"], r["heads_even"], heads_odd, v, h)
        for h in range(heads):
            f_b[v, h + 2] = r["ring"][v, h]
        for side in range(2):
            tile = r["corner_even"][v, 1 - side]
            if corner_odd is not None:
                tile = by_side("ha", tile, corner_odd[v, 1 - side])[side]
            base = heads + 2 if side else 0
            f_b[v, base] = tile
            f_b[v, base + 1] = pltpu.roll(tile, DEPTH, 0)
        pair = []
        for part in range(2):
            before, after = by_side("gx", r["cols_even"][v, part], r["cols_odd"][v, part])
            pair.append(jnp.where(lower, before, after))
        around.append(pair)
        for h in range(-2, heads + 2):
            slot = h + 2
            ring = pltpu.roll(pair[0], cols - DEPTH - SLOT * slot, 1)
            x_a[v, slot] = clamp_cols(plan, f_a[v, h + DEPTH], ring, col_first, col_last)
        for h in range(heads):
            slot = h + 2
            ring = pltpu.roll(pair[1], cols - DEPTH - SLOT * slot, 1)
            x_b[v, h] = clamp_cols(plan, f_b[v, slot], ring, col_first, col_last)

    def block_step(h, main, ring, row_of, x_of, base, store):
        blocks = [main[v, h + base] for v in range(nv)]
        heads_near = [[main[v, h + base + j] for j in range(-2, 3)] for v in range(nv)]
        rows_near = [
            ring_samples(blocks[v], ring[v, row_of(h)], row, 0, rows) for v in range(nv)
        ]
        cols_near = [ring_samples(blocks[v], x_of(v, h), col, 1, cols) for v in range(nv)]
        trig = (r["trig"][0, h + 2], r["trig"][1, h + 2])
        results = advanced(plan, blocks, rows_near, cols_near, heads_near, pace, trig)
        for v in range(nv):
            store(v, h, results[v])

    def put_a(v, h, block):
        s_a[v, h + 2] = block

    def put_b(v, h, block):
        s_b[v, h] = block

    def first_a(i, carry):
        block_step(i - 2, f_a, f_b, lambda h: h + 2, lambda v, h: x_a[v, h + 2], DEPTH, put_a)
        return carry

    def first_b(h, carry):
        block_step(h, f_b, f_a, lambda h: h + DEPTH, lambda v, h: x_b[v, h], 2, put_b)
        return carry

    lax.fori_loop(0, heads + 4, first_a, 0)
    lax.fori_loop(0, heads, first_b, 0)

    faces = []
    for keep_own in (jnp.logical_not(lower), lower):
        mains = [jnp.where(keep_own, r["packed"][v, 0], around[v][0]) for v in range(nv)]
        rings = [jnp.where(keep_own, r["packed"][v, 1], around[v][1]) for v in range(nv)]
        rows_near = [ring_samples(mains[v], rings[v], row, 0, rows) for v in range(nv)]
        shift = lambda block, lanes: pltpu.roll(block, lanes % cols, 1)
        cols_near = [[shift(mains[v], -j) for j in (-2, -1)] + [mains[v]] for v in range(nv)]
        cols_near = [near + [shift(near[2], -j) for j in (1, 2)] for near in cols_near]
        heads_near = [
            [mains[v] if j == 0 else shift(mains[v], -SLOT * j) for j in range(-2, 3)]
            for v in range(nv)
        ]
        trig = (cos_lanes, sin_lanes)
        faces.append(advanced(plan, mains, rows_near, cols_near, heads_near, pace, trig))

    for v in range(nv):
        both = jnp.where(lower, faces[0][v], faces[1][v])
        for h in range(heads):
            own = s_a[v, h + 2]
            ring = pltpu.roll(both, cols - DEPTH - SLOT * (h + 2), 1)
            x_s[v, h] = clamp_cols(plan, own, ring, col_first, col_last)
            s_b[v, h] = clamp_rows(plan, own, s_b[v, h], row_first, row_last)

    def put_out(v, h, block):
        half = 0.5 * (r["value"][v, h] + block)
        r["out"][v, h] = jnp.minimum(half, r["failure"][h])

    def second(h, carry):
        block_step(h, s_a, s_b, lambda h: h, lambda v, h: x_s[v, h], 2, put_out)
        return carry

    lax.fori_loop(0, heads, second, 0)


def local(plan, value, obstacles, obstacle_slots, horizon, speed_offset):
    nv, heads, rows, cols = value.shape
    wide = plan.axes["ha"] > 2
    tile = (rows, cols)

    def turn_swaps(payload):
        blocks = [swap(payload, "ha", False, True)]
        return blocks + [swap(payload, "ha", True, True)] if wide else blocks

    beside = turn_swaps(value)
    half = (nv, heads // 2) + tile
    even_rows, odd_rows = call(pack_rows, plan, [half, half], [value], "v")
    even_rows = swap(even_rows, "gy", False)
    odd_rows = swap(odd_rows, "gy", True)
    (failure,) = call(
        failure_field,
        plan,
        [(heads,) + tile],
        [obstacles, obstacle_slots, horizon, speed_offset],
        "ssss",
    )
    ring, corner = call(
        unpack_rows, plan, [value.shape, (nv, 2) + tile], [value, even_rows, odd_rows], "vvv"
    )
    corners = turn_swaps(corner)
    pack = pack_cols if wide else pack_cols_narrow
    (packed,) = call(
        pack, plan, [(nv, 2) + tile], [value, *beside, ring], "v" * (2 + len(beside))
    )
    even_cols = swap(packed, "gx", False)
    odd_cols = swap(packed, "gx", True)
    args = [value, *beside, ring, *corners, packed, even_cols, odd_cols, failure]
    scratch = [
        pltpu.VMEM((nv, heads + 2 * DEPTH) + tile, jnp.float32),
        pltpu.VMEM((nv, heads + 4) + tile, jnp.float32),
        pltpu.VMEM((nv, heads + 4) + tile, jnp.float32),
        pltpu.VMEM((nv, heads) + tile, jnp.float32),
        pltpu.VMEM((nv, heads + 4) + tile, jnp.float32),
        pltpu.VMEM((nv, heads) + tile, jnp.float32),
        pltpu.VMEM((nv, heads) + tile, jnp.float32),
        pltpu.SMEM((2, heads + 4), jnp.float32),
    ]
    (out,) = call(
        step_kernel,
        plan,
        [value.shape],
        args + [speed_offset],
        "v" * len(args) + "s",
        scratch,
        flops=100000000,
    )
    return out


def pack_cols_narrow(plan, value, heads_even, ring, packed_out):
    pack_cols(plan, value, heads_even, None, ring, packed_out)


def solution(mesh):
    in_specs = (P(None, "ha", "gy", "gx"), P(), P("ha", None), P(), P())
    out_specs = P(None, "ha", "gy", "gx")

    def body(value, *rest):
        return local(Plan(mesh, value.shape), value, *rest)

    return jax.shard_map(body, mesh=mesh, in_specs=in_specs, out_specs=out_specs, check_vma=False)
```

time: 57.1 us -> 30.6 us (0.54)
  the two profiles are of different devices: /device:TPU:1 before, /device:TPU:17 now
where the time goes in v1:
time: 30.6 us; the launch traced here: 30.3 us
  Pallas kernels  12.8 us (42%)
  starting transfers between devices  10.4 us (34%)
  waiting for transfers between devices  3.3 us (11%)
  local copies, waits for them, and re-layouts  2.47 us (8%)
  between operations  1.35 us (4%)
    pallas_call x5, Pallas kernels, call(): pl.pallas_call(functools.partial(body, plan), out_shape=[jax.ShapeDtypeSt...  12.8 us
    ppermute x6, starting transfers between devices, swap(): return lax.ppermute(payload, axis, partners(axis, odd, wrap))  10.4 us
    ppermute x6, waiting for transfers between devices, swap(): return lax.ppermute(payload, axis, partners(axis, odd, wrap))  3.3 us
    unnamed x12, local copies, waits for them, and re-layouts  2.47 us
  transfers between devices with their start and end apart: 6, of which 2 were waited for; matrix products, arithmetic and copies ran while one was open for 0% of the time, Pallas kernels for 24%

profile of v1, /device:TPU:17, one launch (start us, length us, event | category | flops | bytes accessed | tf_op | source)
XLA Modules:
  0.0 30.3 jit_solution(15580629293159349503)
XLA Ops:
  0.0 1.2 %collective-permute-start = (f32[4,8,8,128]{3,2,1,0:T(8,128)}, f32[4,8,8,128]{3,2,1,0:T(8,128)S(1)}, u32[]{:S(2)}, u32[]{:S(2)}) collective-permute-start(f32[4,8,8,128]{3,2,1,0:T(8,128)} %refs_0_.1), channel_id=1, source_target_pairs={{0,1},{1,0},{2,3},{3,2},{4,5},{5,4},{6,7},{7,6},{8,9},{9,8},{10,11... | collective-permute-start | bytes 393224 | tf_op jit(solution)/shard_map/ppermute | solution.py:82
  1.2 1.6 %pack_rows.1 = (f32[4,4,8,128]{3,2,1,0:T(8,128)}, f32[4,4,8,128]{3,2,1,0:T(8,128)}) custom-call(f32[4,8,8,128]{3,2,1,0:T(8,128)} %refs_0_.1), custom_call_target="tpu_custom_call" | custom-call | flops 1000000 | bytes 400000 | tf_op jit(solution)/shard_map/pack_rows/pallas_call | solution.py:100
  2.8 1.3 %collective-permute-start.1 = (f32[4,4,8,128]{3,2,1,0:T(8,128)}, f32[4,4,8,128]{3,2,1,0:T(8,128)S(1)}, u32[]{:S(2)}, u32[]{:S(2)}) collective-permute-start(f32[4,4,8,128]{3,2,1,0:T(8,128)} %get-tuple-element.9), channel_id=1, source_target_pairs={{0,2},{2,0},{4,6},{6,4},{1,3},{3,1},{5,7},{7,5},{8,10},{10,8},{12,... | collective-permute-start | bytes 196616 | tf_op jit(solution)/shard_map/ppermute | solution.py:82
  4.1 1.9 %collective-permute-start.2 = (f32[4,4,8,128]{3,2,1,0:T(8,128)}, f32[4,4,8,128]{3,2,1,0:T(8,128)S(1)}, u32[]{:S(2)}, u32[]{:S(2)}) collective-permute-start(f32[4,4,8,128]{3,2,1,0:T(8,128)} %get-tuple-element.10), channel_id=1, source_target_pairs={{2,4},{4,2},{3,5},{5,3},{10,12},{12,10},{11,13},{13,11},{18,20},{2... | collective-permute-start | bytes 196616 | tf_op jit(solution)/shard_map/ppermute | solution.py:82
  6.0 0.1 collective-permute-done.1.even_in
  6.1 0.0 copy-start.1
  6.1 3.2 %collective-permute-done.2.odd_in = f32[4,4,8,128]{3,2,1,0:T(8,128)S(1)} collective-permute-done((f32[4,4,8,128]{3,2,1,0:T(8,128)}, f32[4,4,8,128]{3,2,1,0:T(8,128)S(1)}, u32[]{:S(2)}, u32[]{:S(2)}) %collective-permute-start.2) | collective-permute-done | bytes 65568 | tf_op jit(solution)/shard_map/ppermute | solution.py:82
  9.3 0.0 copy-done.1
  9.3 0.0 copy-start.2
  9.3 0.6 %copy-done.2 = f32[4,4,8,128]{3,2,1,0:T(8,128)} copy-done((f32[4,4,8,128]{3,2,1,0:T(8,128)}, f32[4,4,8,128]{3,2,1,0:T(8,128)S(1)}, u32[]{:S(2)}) %copy-start.2) | copy-done | bytes 65560
  9.9 1.6 %unpack_rows.1 = (f32[4,8,8,128]{3,2,1,0:T(8,128)}, f32[4,2,8,128]{3,2,1,0:T(8,128)}) custom-call(f32[4,8,8,128]{3,2,1,0:T(8,128)} %refs_0_.1, f32[4,4,8,128]{3,2,1,0:T(8,128)} %copy-done.1, f32[4,4,8,128]{3,2,1,0:T(8,128)} %copy-done.2), custom_call_target="tpu_custom_call" | custom-call | flops 1000000 | bytes 400000 | tf_op jit(solution)/shard_map/unpack_rows/pallas_call | solution.py:100
  11.6 0.3 collective-permute-start.3
  11.8 0.0 collective-permute-done.heads_even.refs_1_
  11.8 0.0 copy-start
  11.8 0.6 %copy-done = f32[4,8,8,128]{3,2,1,0:T(8,128)} copy-done((f32[4,8,8,128]{3,2,1,0:T(8,128)}, f32[4,8,8,128]{3,2,1,0:T(8,128)S(1)}, u32[]{:S(2)}) %copy-start) | copy-done | bytes 131096
  12.5 1.8 %pack_cols_narrow.1.refs_4_ = f32[4,2,8,128]{3,2,1,0:T(8,128)} custom-call(f32[4,8,8,128]{3,2,1,0:T(8,128)} %refs_0_.1, f32[4,8,8,128]{3,2,1,0:T(8,128)} %copy-done, f32[4,8,8,128]{3,2,1,0:T(8,128)} %get-tuple-element.11.ring.refs_2_), custom_call_target="tpu_custom_call" | custom-call | flops 1000000 | bytes 400000 | tf_op jit(solution)/shard_map/pack_cols_narrow/pallas_call | solution.py:100
  14.3 5.7 %collective-permute-start.5 = (f32[4,2,8,128]{3,2,1,0:T(8,128)}, f32[4,2,8,128]{3,2,1,0:T(8,128)S(1)}, u32[]{:S(2)}, u32[]{:S(2)}) collective-permute-start(f32[4,2,8,128]{3,2,1,0:T(8,128)} %pack_cols_narrow.1.refs_4_), channel_id=1, source_target_pairs={{8,16},{16,8},{9,17},{17,9},{10,18},{18,10},{11,19},{19,11},{12,20... | collective-permute-start | bytes 98312 | tf_op jit(solution)/shard_map/ppermute | solution.py:82
  20.0 0.1 collective-permute-start.4
  21.3 2.1 %failure_field.1.refs_7_ = f32[8,8,128]{2,1,0:T(8,128)} custom-call(f32[5,128]{1,0:T(8,128)} %obstacles.1, s32[2,16]{1,0:T(2,128)} %slots.1, f32[1]{0:T(128)S(6)} %copy.6.horizon, s32[1]{0:T(128)S(6)} %copy.7.offset.refs_8_), custom_call_target="tpu_custom_call" | custom-call | flops 1000000 | bytes 400000 | tf_op jit(solution)/shard_map/failure_field/pallas_call | solution.py:100
  23.4 0.0 collective-permute-done.3.refs_3_
  23.4 0.0 copy-start.3
  23.4 0.0 collective-permute-done.5.refs_6_
  23.5 0.0 copy-start.4
  23.5 0.0 collective-permute-done.4.refs_5_
  23.5 0.6 %copy-done.3 = f32[4,2,8,128]{3,2,1,0:T(8,128)} copy-done((f32[4,2,8,128]{3,2,1,0:T(8,128)}, f32[4,2,8,128]{3,2,1,0:T(8,128)S(1)}, u32[]{:S(2)}) %copy-start.3) | copy-done | bytes 32792
  24.1 0.0 copy-done.4
  24.1 0.0 copy-start.5
  24.1 0.6 %copy-done.5 = f32[4,2,8,128]{3,2,1,0:T(8,128)} copy-done((f32[4,2,8,128]{3,2,1,0:T(8,128)}, f32[4,2,8,128]{3,2,1,0:T(8,128)S(1)}, u32[]{:S(2)}) %copy-start.5) | copy-done | bytes 32792
  24.7 5.6 %step_kernel.1 = f32[4,8,8,128]{3,2,1,0:T(8,128)} custom-call(f32[4,8,8,128]{3,2,1,0:T(8,128)} %refs_0_.1, f32[4,8,8,128]{3,2,1,0:T(8,128)} %copy-done, f32[4,8,8,128]{3,2,1,0:T(8,128)} %get-tuple-element.11.ring.refs_2_, f32[4,2,8,128]{3,2,1,0:T(8,128)} %copy-done.3, f32[4,2,8,128]{3,2,1,0:T(8,128)} %pack_cols_narrow.1.refs_4_, f32[4,2,8,128]{3,2,1,0:T(8,128)} %copy-done.5, ...), custom_call_target="tpu_custom_call" | custom-call | flops 100000000 | bytes 400000 | tf_op jit(solution)/shard_map/step_kernel/pallas_call | solution.py:100
Async XLA Ops:
  0.0 11.8 %collective-permute-start = (f32[4,8,8,128]{3,2,1,0:T(8,128)}, f32[4,8,8,128]{3,2,1,0:T(8,128)S(1)}, u32[]{:S(2)}, u32[]{:S(2)}) collective-permute-start(f32[4,8,8,128]{3,2,1,0:T(8,128)} %refs_0_.1), channel_id=1, source_target_pairs={{0,1},{1,0},{2,3},{3,2},{4,5},{5,4},{6,7},{7,6},{8,9},{9,8},{10,11... | collective-permute-start | bytes 393224 | tf_op jit(solution)/shard_map/ppermute | solution.py:82
  2.8 3.3 %collective-permute-start.1 = (f32[4,4,8,128]{3,2,1,0:T(8,128)}, f32[4,4,8,128]{3,2,1,0:T(8,128)S(1)}, u32[]{:S(2)}, u32[]{:S(2)}) collective-permute-start(f32[4,4,8,128]{3,2,1,0:T(8,128)} %get-tuple-element.9), channel_id=1, source_target_pairs={{0,2},{2,0},{4,6},{6,4},{1,3},{3,1},{5,7},{7,5},{8,10},{10,8},{12,... | collective-permute-start | bytes 196616 | tf_op jit(solution)/shard_map/ppermute | solution.py:82
  4.1 5.2 %collective-permute-start.2 = (f32[4,4,8,128]{3,2,1,0:T(8,128)}, f32[4,4,8,128]{3,2,1,0:T(8,128)S(1)}, u32[]{:S(2)}, u32[]{:S(2)}) collective-permute-start(f32[4,4,8,128]{3,2,1,0:T(8,128)} %get-tuple-element.10), channel_id=1, source_target_pairs={{2,4},{4,2},{3,5},{5,3},{10,12},{12,10},{11,13},{13,11},{18,20},{2... | collective-permute-start | bytes 196616 | tf_op jit(solution)/shard_map/ppermute | solution.py:82
  6.1 3.2 %copy-start.1 = (f32[4,4,8,128]{3,2,1,0:T(8,128)}, f32[4,4,8,128]{3,2,1,0:T(8,128)S(1)}, u32[]{:S(2)}) copy-start(f32[4,4,8,128]{3,2,1,0:T(8,128)S(1)} %collective-permute-done.1.even_in) | copy-start | bytes 196612
  9.3 0.6 %copy-start.2 = (f32[4,4,8,128]{3,2,1,0:T(8,128)}, f32[4,4,8,128]{3,2,1,0:T(8,128)S(1)}, u32[]{:S(2)}) copy-start(f32[4,4,8,128]{3,2,1,0:T(8,128)S(1)} %collective-permute-done.2.odd_in) | copy-start | bytes 196612
  11.6 11.9 %collective-permute-start.3 = (f32[4,2,8,128]{3,2,1,0:T(8,128)}, f32[4,2,8,128]{3,2,1,0:T(8,128)S(1)}, u32[]{:S(2)}, u32[]{:S(2)}) collective-permute-start(f32[4,2,8,128]{3,2,1,0:T(8,128)} %get-tuple-element.12), channel_id=1, source_target_pairs={{0,1},{1,0},{2,3},{3,2},{4,5},{5,4},{6,7},{7,6},{8,9},{9,8},{10,11... | collective-permute-start | bytes 98312 | tf_op jit(solution)/shard_map/ppermute | solution.py:82
  11.8 0.6 %copy-start = (f32[4,8,8,128]{3,2,1,0:T(8,128)}, f32[4,8,8,128]{3,2,1,0:T(8,128)S(1)}, u32[]{:S(2)}) copy-start(f32[4,8,8,128]{3,2,1,0:T(8,128)S(1)} %collective-permute-done.heads_even.refs_1_) | copy-start | bytes 393220
  14.3 9.2 %collective-permute-start.5 = (f32[4,2,8,128]{3,2,1,0:T(8,128)}, f32[4,2,8,128]{3,2,1,0:T(8,128)S(1)}, u32[]{:S(2)}, u32[]{:S(2)}) collective-permute-start(f32[4,2,8,128]{3,2,1,0:T(8,128)} %pack_cols_narrow.1.refs_4_), channel_id=1, source_target_pairs={{8,16},{16,8},{9,17},{17,9},{10,18},{18,10},{11,19},{19,11},{12,20... | collective-permute-start | bytes 98312 | tf_op jit(solution)/shard_map/ppermute | solution.py:82
  20.0 3.5 %collective-permute-start.4 = (f32[4,2,8,128]{3,2,1,0:T(8,128)}, f32[4,2,8,128]{3,2,1,0:T(8,128)S(1)}, u32[]{:S(2)}, u32[]{:S(2)}) collective-permute-start(f32[4,2,8,128]{3,2,1,0:T(8,128)} %pack_cols_narrow.1.refs_4_), channel_id=1, source_target_pairs={{0,8},{8,0},{16,24},{24,16},{1,9},{9,1},{17,25},{25,17},{2,10},{10... | collective-permute-start | bytes 98312 | tf_op jit(solution)/shard_map/ppermute | solution.py:82
  23.4 0.6 %copy-start.3 = (f32[4,2,8,128]{3,2,1,0:T(8,128)}, f32[4,2,8,128]{3,2,1,0:T(8,128)S(1)}, u32[]{:S(2)}) copy-start(f32[4,2,8,128]{3,2,1,0:T(8,128)S(1)} %collective-permute-done.3.refs_3_) | copy-start | bytes 98308
  23.5 0.6 %copy-start.4 = (f32[4,2,8,128]{3,2,1,0:T(8,128)}, f32[4,2,8,128]{3,2,1,0:T(8,128)S(1)}, u32[]{:S(2)}) copy-start(f32[4,2,8,128]{3,2,1,0:T(8,128)S(1)} %collective-permute-done.5.refs_6_) | copy-start | bytes 98308
  24.1 0.6 %copy-start.5 = (f32[4,2,8,128]{3,2,1,0:T(8,128)}, f32[4,2,8,128]{3,2,1,0:T(8,128)S(1)}, u32[]{:S(2)}) copy-start(f32[4,2,8,128]{3,2,1,0:T(8,128)S(1)} %collective-permute-done.4.refs_5_) | copy-start | bytes 98308

commit v2 on v1

--- a/solution.py
+++ b/solution.py
@@ -68,18 +68,19 @@
         return speeds, (top * self.most_cos, top * self.most_sin), time_step
 
 
-def partners(axis, odd, wrap):
+def swap(payload, axis, odd, wrap=False):
     count = lax.axis_size(axis)
+    if axis != "gy" or not odd or wrap:
+        first = 1 if odd else 0
+        pairs = [(i, (i + 1) % count) for i in range(first, count, 2)]
+        return lax.ppermute(payload, axis, pairs + [(j, i) for i, j in pairs])
     pairs = []
-    for i in range(1 if odd else 0, count, 2):
-        j = i + 1
-        if j < count or wrap:
-            pairs += [(i, j % count), (j % count, i)]
-    return pairs
-
-
-def swap(payload, axis, odd, wrap=False):
-    return lax.ppermute(payload, axis, partners(axis, odd, wrap))
+    for x in range(lax.axis_size("gx")):
+        for y in range(count):
+            end = y in (0, count - 1)
+            there = (x ^ 1, y) if end else (x, y + 1 if y % 2 else y - 1)
+            pairs.append((x * count + y, there[0] * count + there[1]))
+    return lax.ppermute(payload, ("gx", axis), pairs)
 
 
 def by_side(axis, even_block, odd_block):
@@ -96,7 +97,7 @@
 
 
 def call(body, plan, out_shapes, args, specs, scratch=(), flops=1000000):
-    space = {"v": pltpu.VMEM, "s": pltpu.SMEM}
+    space = {"v": pltpu.VMEM, "s": pltpu.SMEM, "a": pl.ANY}
     return pl.pallas_call(
         functools.partial(body, plan),
         out_shape=[jax.ShapeDtypeStruct(shape, jnp.float32) for shape in out_shapes],
@@ -105,6 +106,7 @@
         scratch_shapes=scratch,
         name=body.__name__,
         cost_estimate=pl.CostEstimate(flops=flops, bytes_accessed=400000, transcendentals=0),
+        compiler_params=pltpu.CompilerParams(vmem_limit_bytes=8 * 2**20),
     )(*args)
 
 
@@ -124,7 +126,7 @@
             odd_out[v, pair] = jnp.where(is_even, low, high)
 
 
-def unpack_rows(plan, value, even_in, odd_in, ring_out, corner_out):
+def unpack_rows(plan, value, even_in, odd_in, _, ring_out, corner_out):
     row = iota(plan, 0)
     at_first = jnp.logical_and(row >= DEPTH, is_first("gy"))
     at_last = jnp.logical_and(row < DEPTH, is_last("gy"))
@@ -438,7 +440,7 @@
         "ssss",
     )
     ring, corner = call(
-        unpack_rows, plan, [value.shape, (nv, 2) + tile], [value, even_rows, odd_rows], "vvv"
+        unpack_rows, plan, [value.shape, (nv, 2) + tile], [value, even_rows, odd_rows, failure], "vvva"
     )
     corners = turn_swaps(corner)
     pack = pack_cols if wide else pack_cols_narrow

time: 30.6 us -> 17.9 us (0.58)
  Pallas kernels: 12.8 us -> 6.13 us
  starting transfers between devices: 10.4 us -> 6.46 us
  local copies, waits for them, and re-layouts: 2.47 us -> 0.95 us
  waiting for transfers between devices: 3.3 us -> 2.79 us
    pallas_call x5, Pallas kernels: 12.8 us -> 6.13 us  [call(): pl.pallas_call(functools.partial(body, plan), out_shape=[jax.ShapeDtypeSt...]
    ppermute x6, starting transfers between devices: 10.4 us -> 6.46 us  [the longest x5 6.46 us: swap(): return lax.ppermute(payload, axis, pairs + [(j, i) for i, j in pairs])]
    unnamed x12 -> x8, local copies, waits for them, and re-layouts: 2.47 us -> 0.95 us
    ppermute x6, waiting for transfers between devices: 3.3 us -> 2.79 us  [the longest x5 2.1 us: swap(): return lax.ppermute(payload, axis, pairs + [(j, i) for i, j in pairs])]
  transfers between devices with their start and end apart: 6 -> 6, of which waited for: 2 -> 2; matrix products, arithmetic and copies ran while one was open for 0% -> 0% of each run, Pallas kernels for 24% -> 9%
where the time goes in v2:
time: 17.9 us; the launch traced here: 17.7 us
  starting transfers between devices  6.46 us (36%)
  Pallas kernels  6.13 us (34%)
  waiting for transfers between devices  2.79 us (16%)
  between operations  1.38 us (8%)
  local copies, waits for them, and re-layouts  0.95 us (5%)
    ppermute x5, starting transfers between devices, swap(): return lax.ppermute(payload, axis, pairs + [(j, i) for i, j in pairs])  6.46 us
    pallas_call x5, Pallas kernels, call(): pl.pallas_call(functools.partial(body, plan), out_shape=[jax.ShapeDtypeSt...  6.13 us
    ppermute x5, waiting for transfers between devices, swap(): return lax.ppermute(payload, axis, pairs + [(j, i) for i, j in pairs])  2.1 us
    unnamed x8, local copies, waits for them, and re-layouts  0.95 us
    ppermute x1, waiting for transfers between devices, swap(): return lax.ppermute(payload, ('gx', axis), pairs)  0.69 us
  transfers between devices with their start and end apart: 6, of which 2 were waited for; matrix products, arithmetic and copies ran while one was open for 0% of the time, Pallas kernels for 9%

profile of v2, /device:TPU:17, one launch (start us, length us, event | category | flops | bytes accessed | tf_op | source)
XLA Modules:
  0.0 17.7 jit_solution(15978936667210828670)
XLA Ops:
  0.0 1.2 %collective-permute-start = (f32[4,8,8,128]{3,2,1,0:T(8,128)}, f32[4,8,8,128]{3,2,1,0:T(8,128)S(1)}, u32[]{:S(2)}, u32[]{:S(2)}) collective-permute-start(f32[4,8,8,128]{3,2,1,0:T(8,128)} %refs_0_.1), channel_id=1, source_target_pairs={{0,1},{1,0},{2,3},{3,2},{4,5},{5,4},{6,7},{7,6},{8,9},{9,8},{10,11... | collective-permute-start | bytes 393224 | tf_op jit(solution)/shard_map/ppermute | solution.py:76
  1.2 0.0 copy-start
  1.2 0.9 %copy-done = f32[4,8,8,128]{3,2,1,0:T(8,128)S(1)} copy-done((f32[4,8,8,128]{3,2,1,0:T(8,128)S(1)}, f32[4,8,8,128]{3,2,1,0:T(8,128)}, u32[]{:S(2)}) %copy-start) | copy-done | bytes 131096
  2.2 0.0 copy-start.1
  2.2 0.0 copy-start.2
  2.2 1.4 %collective-permute-start.1 = (f32[4,4,8,128]{3,2,1,0:T(8,128)S(1)}, f32[4,4,8,128]{3,2,1,0:T(8,128)S(1)}, u32[]{:S(2)}, u32[]{:S(2)}) collective-permute-start(f32[4,4,8,128]{3,2,1,0:T(8,128)S(1)} %get-tuple-element.9), channel_id=1, source_target_pairs={{0,2},{4,6},{2,0},{6,4},{1,3},{5,7},{3,1},{7,5},{8,10},{12,14},{10... | collective-permute-start | bytes 196616 | tf_op jit(solution)/shard_map/ppermute | solution.py:76
  3.6 0.0 collective-permute-start.2
  4.2 0.0 copy-start.3
  4.9 0.0 copy-done.2
  4.9 0.0 copy-done.3
  4.9 1.4 %failure_field.1._.refs_7_ = f32[8,8,128]{2,1,0:T(8,128)S(1)} custom-call(f32[5,128]{1,0:T(8,128)S(1)} %copy-done.2, s32[2,16]{1,0:T(2,128)S(1)} %copy-done.3, f32[1]{0:T(128)S(6)} %copy.6.horizon, s32[1]{0:T(128)S(6)} %copy.7.offset.refs_8_), custom_call_target="tpu_custom_call" | custom-call | flops 1000000 | bytes 400000 | tf_op jit(solution)/shard_map/failure_field/pallas_call | solution.py:101
  6.3 0.0 collective-permute-done.1.even_in
  6.3 0.7 %collective-permute-done.2.odd_in = f32[4,4,8,128]{3,2,1,0:T(8,128)S(1)} collective-permute-done((f32[4,4,8,128]{3,2,1,0:T(8,128)S(1)}, f32[4,4,8,128]{3,2,1,0:T(8,128)S(1)}, u32[]{:S(2)}, u32[]{:S(2)}) %collective-permute-start.2) | collective-permute-done | bytes 65568 | tf_op jit(solution)/shard_map/ppermute | solution.py:83
  7.0 0.0 copy-done.1
  7.0 0.3 %collective-permute-start.3 = (f32[4,2,8,128]{3,2,1,0:T(8,128)S(1)}, f32[4,2,8,128]{3,2,1,0:T(8,128)S(1)}, u32[]{:S(2)}, u32[]{:S(2)}) collective-permute-start(f32[4,2,8,128]{3,2,1,0:T(8,128)S(1)} %get-tuple-element.12), channel_id=1, source_target_pairs={{0,1},{1,0},{2,3},{3,2},{4,5},{5,4},{6,7},{7,6},{8,9},{9,8},{10,11... | collective-permute-start | bytes 98312 | tf_op jit(solution)/shard_map/ppermute | solution.py:76
  7.3 0.0 collective-permute-done.heads_even.refs_1_
  7.3 0.2 pack_cols_narrow.1.refs_4_
  7.5 3.6 %collective-permute-start.5 = (f32[4,2,8,128]{3,2,1,0:T(8,128)S(1)}, f32[4,2,8,128]{3,2,1,0:T(8,128)S(1)}, u32[]{:S(2)}, u32[]{:S(2)}) collective-permute-start(f32[4,2,8,128]{3,2,1,0:T(8,128)S(1)} %pack_cols_narrow.1.refs_4_), channel_id=1, source_target_pairs={{8,16},{24,0},{16,8},{0,24},{9,17},{25,1},{17,9},{1,25},{10,18},{2... | collective-permute-start | bytes 98312 | tf_op jit(solution)/shard_map/ppermute | solution.py:76
  11.1 0.0 collective-permute-start.4
  11.1 0.0 collective-permute-done.3.refs_3_
  11.1 2.1 %collective-permute-done.5.refs_6_ = f32[4,2,8,128]{3,2,1,0:T(8,128)S(1)} collective-permute-done((f32[4,2,8,128]{3,2,1,0:T(8,128)S(1)}, f32[4,2,8,128]{3,2,1,0:T(8,128)S(1)}, u32[]{:S(2)}, u32[]{:S(2)}) %collective-permute-start.5) | collective-permute-done | bytes 32800 | tf_op jit(solution)/shard_map/ppermute | solution.py:76
  13.1 0.0 collective-permute-done.4.refs_5_
  13.2 4.6 %step_kernel.1 = f32[4,8,8,128]{3,2,1,0:T(8,128)} custom-call(f32[4,8,8,128]{3,2,1,0:T(8,128)S(1)} %copy-done.1, f32[4,8,8,128]{3,2,1,0:T(8,128)S(1)} %collective-permute-done.heads_even.refs_1_, f32[4,8,8,128]{3,2,1,0:T(8,128)S(1)} %get-tuple-element.11.ring.refs_2_, f32[4,2,8,128]{3,2,1,0:T(8,128)S(1)} %collective-permute-done.3.refs_3_, ...), custom_call_target="tpu_custom_call" | custom-call | flops 100000000 | bytes 400000 | tf_op jit(solution)/shard_map/step_kernel/pallas_call | solution.py:101
  (2 shorter events, 0.1 us)
Async XLA Ops:
  0.0 7.3 %collective-permute-start = (f32[4,8,8,128]{3,2,1,0:T(8,128)}, f32[4,8,8,128]{3,2,1,0:T(8,128)S(1)}, u32[]{:S(2)}, u32[]{:S(2)}) collective-permute-start(f32[4,8,8,128]{3,2,1,0:T(8,128)} %refs_0_.1), channel_id=1, source_target_pairs={{0,1},{1,0},{2,3},{3,2},{4,5},{5,4},{6,7},{7,6},{8,9},{9,8},{10,11... | collective-permute-start | bytes 393224 | tf_op jit(solution)/shard_map/ppermute | solution.py:76
  1.2 0.9 %copy-start = (f32[4,8,8,128]{3,2,1,0:T(8,128)S(1)}, f32[4,8,8,128]{3,2,1,0:T(8,128)}, u32[]{:S(2)}) copy-start(f32[4,8,8,128]{3,2,1,0:T(8,128)} %refs_0_.1) | copy-start | bytes 393220
  2.2 4.8 %copy-start.1 = (f32[4,8,8,128]{3,2,1,0:T(8,128)S(1)}, f32[4,8,8,128]{3,2,1,0:T(8,128)}, u32[]{:S(2)}) copy-start(f32[4,8,8,128]{3,2,1,0:T(8,128)} %refs_0_.1) | copy-start | bytes 393220
  2.2 2.7 %copy-start.2 = (f32[5,128]{1,0:T(8,128)S(1)}, f32[5,128]{1,0:T(8,128)}, u32[]{:S(2)}) copy-start(f32[5,128]{1,0:T(8,128)} %obstacles.1) | copy-start | bytes 7684
  2.2 4.1 %collective-permute-start.1 = (f32[4,4,8,128]{3,2,1,0:T(8,128)S(1)}, f32[4,4,8,128]{3,2,1,0:T(8,128)S(1)}, u32[]{:S(2)}, u32[]{:S(2)}) collective-permute-start(f32[4,4,8,128]{3,2,1,0:T(8,128)S(1)} %get-tuple-element.9), channel_id=1, source_target_pairs={{0,2},{4,6},{2,0},{6,4},{1,3},{5,7},{3,1},{7,5},{8,10},{12,14},{10... | collective-permute-start | bytes 196616 | tf_op jit(solution)/shard_map/ppermute | solution.py:76
  3.6 3.4 %collective-permute-start.2 = (f32[4,4,8,128]{3,2,1,0:T(8,128)S(1)}, f32[4,4,8,128]{3,2,1,0:T(8,128)S(1)}, u32[]{:S(2)}, u32[]{:S(2)}) collective-permute-start(f32[4,4,8,128]{3,2,1,0:T(8,128)S(1)} %get-tuple-element.10), channel_id=1, source_target_pairs={{0,8},{2,4},{4,2},{6,14},{8,0},{10,12},{12,10},{14,6},{16,24},{18,... | collective-permute-start | bytes 196616 | tf_op jit(solution)/shard_map/ppermute | solution.py:83
  4.2 0.7 %copy-start.3 = (s32[2,16]{1,0:T(2,128)S(1)}, s32[2,16]{1,0:T(2,128)}, u32[]{:S(2)}) copy-start(s32[2,16]{1,0:T(2,128)} %slots.1) | copy-start | bytes 388
  7.0 4.0 %collective-permute-start.3 = (f32[4,2,8,128]{3,2,1,0:T(8,128)S(1)}, f32[4,2,8,128]{3,2,1,0:T(8,128)S(1)}, u32[]{:S(2)}, u32[]{:S(2)}) collective-permute-start(f32[4,2,8,128]{3,2,1,0:T(8,128)S(1)} %get-tuple-element.12), channel_id=1, source_target_pairs={{0,1},{1,0},{2,3},{3,2},{4,5},{5,4},{6,7},{7,6},{8,9},{9,8},{10,11... | collective-permute-start | bytes 98312 | tf_op jit(solution)/shard_map/ppermute | solution.py:76
  7.5 5.7 %collective-permute-start.5 = (f32[4,2,8,128]{3,2,1,0:T(8,128)S(1)}, f32[4,2,8,128]{3,2,1,0:T(8,128)S(1)}, u32[]{:S(2)}, u32[]{:S(2)}) collective-permute-start(f32[4,2,8,128]{3,2,1,0:T(8,128)S(1)} %pack_cols_narrow.1.refs_4_), channel_id=1, source_target_pairs={{8,16},{24,0},{16,8},{0,24},{9,17},{25,1},{17,9},{1,25},{10,18},{2... | collective-permute-start | bytes 98312 | tf_op jit(solution)/shard_map/ppermute | solution.py:76
  11.1 2.1 %collective-permute-start.4 = (f32[4,2,8,128]{3,2,1,0:T(8,128)S(1)}, f32[4,2,8,128]{3,2,1,0:T(8,128)S(1)}, u32[]{:S(2)}, u32[]{:S(2)}) collective-permute-start(f32[4,2,8,128]{3,2,1,0:T(8,128)S(1)} %pack_cols_narrow.1.refs_4_), channel_id=1, source_target_pairs={{0,8},{16,24},{8,0},{24,16},{1,9},{17,25},{9,1},{25,17},{2,10},{18... | collective-permute-start | bytes 98312 | tf_op jit(solution)/shard_map/ppermute | solution.py:76

commit v3 on v2

--- a/solution.py
+++ b/solution.py
@@ -153,27 +153,26 @@
     return jnp.where(at_last, jnp.broadcast_to(own[plan.rows - 1 :], shape), ring)
 
 
-def clamp_cols(plan, own, ring, at_first, at_last):
-    shape = (plan.rows, plan.cols)
-    ring = jnp.where(at_first, jnp.broadcast_to(own[:, 0:1], shape), ring)
-    return jnp.where(at_last, jnp.broadcast_to(own[:, plan.cols - 1 :], shape), ring)
-
-
-def pack_cols(plan, value, heads_even, heads_odd, ring, packed_out):
-    slot_id = iota(plan, 1) // SLOT
+def pack_cols(plan, value, heads_even, heads_odd, ring, packed_out, even_out, odd_out):
+    col = iota(plan, 1)
+    lower = col % SLOT < DEPTH
+    slot_id = col // SLOT
+    is_even = lax.axis_index("gx") % 2 == 0
     for v in range(plan.speeds):
-        packed = jnp.zeros((plan.rows, plan.cols), jnp.float32)
+        main = jnp.zeros((plan.rows, plan.cols), jnp.float32)
         for h in range(-2, plan.heads + 2):
             block = head_block(plan, value, heads_even, heads_odd, v, h)
-            slot = h + 2
-            packed = jnp.where(slot_id == slot, pltpu.roll(block, DEPTH + SLOT * slot, 1), packed)
-        packed_out[v, 0] = packed
-        packed = jnp.zeros((plan.rows, plan.cols), jnp.float32)
+            main = jnp.where(slot_id == h + 2, pltpu.roll(block, DEPTH + SLOT * (h + 2), 1), main)
+        outer = jnp.zeros((plan.rows, plan.cols), jnp.float32)
         for h in range(plan.heads):
-            slot = h + 2
-            moved = pltpu.roll(ring[v, h], DEPTH + SLOT * slot, 1)
-            packed = jnp.where(slot_id == slot, moved, packed)
-        packed_out[v, 1] = packed
+            moved = pltpu.roll(ring[v, h], DEPTH + SLOT * (h + 2), 1)
+            outer = jnp.where(slot_id == h + 2, moved, outer)
+        packed_out[v, 0] = main
+        packed_out[v, 1] = outer
+        last = jnp.where(lower, main, pltpu.roll(outer, DEPTH, 1))
+        first = jnp.where(lower, pltpu.roll(main, plan.cols - DEPTH, 1), outer)
+        even_out[v] = jnp.where(is_even, last, first)
+        odd_out[v] = jnp.where(is_even, first, last)
 
 
 def head_block(plan, value, heads_even, heads_odd, v, h):
@@ -229,190 +228,336 @@
     return t * t
 
 
-def sides_of(bends, floor):
-    before, here, after = bends
-    half = 0.5 * sharp(here, floor)
-    low = half + sharp(before, floor)
-    high = half + sharp(after, floor)
-    return (before - here) * high, (after - here) * low, half / (low * high)
-
-
-def bends_of(samples):
-    steps = [samples[i + 1] - samples[i] for i in range(4)]
-    return [steps[i + 1] - steps[i] for i in range(3)], samples[3] - samples[1]
-
-
-def drift_term(samples, floor, drift, spread, spacing):
-    bends, across = bends_of(samples)
-    a, b, r = sides_of(bends, floor)
+def sides_of(bends, weights):
+    half = 0.5 * weights[1]
+    low = half + weights[0]
+    high = half + weights[2]
+    return (bends[0] - bends[1]) * high, (bends[2] - bends[1]) * low, half / (low * high)
+
+
+def drift_term(across, bends, weights, drift, spread, spacing):
+    a, b, r = sides_of(bends, weights)
     quarter = 0.25 / spacing
     return (drift * (0.5 / spacing)) * across + r * (
         ((spread + drift) * quarter) * a + ((spread - drift) * quarter) * b
     )
 
 
-def limit_term(bends, across, floor, limit, spacing):
-    a, b, r = sides_of(bends, floor)
+def limit_term(across, bends, weights, limit, spacing):
+    a, b, r = sides_of(bends, weights)
     r = r * (0.25 * limit / spacing)
     return jnp.abs((0.5 * limit / spacing) * across + r * (a - b)) + r * (a + b)
 
 
-def ring_samples(block, ring, place, axis, length):
-    return [
-        pltpu.roll(jnp.where(place >= length - 2, ring, block), 2, axis),
-        pltpu.roll(jnp.where(place >= length - 1, ring, block), 1, axis),
-        block,
-        pltpu.roll(jnp.where(place < 1, ring, block), length - 1, axis),
-        pltpu.roll(jnp.where(place < 2, ring, block), length - 2, axis),
-    ]
-
-
-def speed_terms(plan, blocks):
+def bend_of(before, here, after):
+    return (after - here) - (here - before)
+
+
+def stencil(samples, floor):
+    bends = [bend_of(*samples[i : i + 3]) for i in range(3)]
+    return samples[3] - samples[1], bends, [sharp(bend, floor) for bend in bends]
+
+
+class Shifts:
+    def __init__(self, plan, axis):
+        self.axis = axis
+        self.length = (plan.rows, plan.cols)[axis]
+        place = iota(plan, axis)
+        self.ends = {-1: place >= self.length - 1, -2: place >= self.length - 2}
+        self.ends.update({1: place < 1, 2: place < 2})
+
+    def at(self, block, ring, offset):
+        merged = jnp.where(self.ends[offset], ring, block)
+        return pltpu.roll(merged, -offset % self.length, self.axis)
+
+    def both(self, block, ring):
+        return self.at(block, ring, -1), self.at(block, ring, 1)
+
+    def samples(self, block, ring):
+        return [block if j == 0 else self.at(block, ring, j) for j in range(-2, 3)]
+
+    def turned(self, block, stride=1):
+        shift = lambda j: pltpu.roll(block, -stride * j % self.length, self.axis)
+        return [block if j == 0 else shift(j) for j in range(-2, 3)]
+
+    def near(self, block, ring, floor):
+        before, after = self.both(block, ring)
+        bend = bend_of(before, block, after)
+        return after - before, bend, sharp(bend, floor)
+
+    def stencil(self, near, ring_bend, ring_weight):
+        across, bend, weight = near
+        bends = self.both(bend, ring_bend)
+        weights = self.both(weight, ring_weight)
+        return across, [bends[0], bend, bends[1]], [weights[0], weight, weights[1]]
+
+
+def speed_terms(blocks):
     floor = weno_eps * speed_step * speed_step
     count = len(blocks)
     at = lambda k: blocks[min(max(k, 0), count - 1)]
-    steps = {k: at(k + 1) - at(k) for k in range(0, count - 1)}
     zero = jnp.zeros_like(blocks[0])
-    step = lambda k: steps.get(k, zero)
-    terms = []
-    for k in range(count):
-        bends = [step(k + j) - step(k + j - 1) for j in (-1, 0, 1)]
-        terms.append(limit_term(bends, at(k + 1) - at(k - 1), floor, accel_limit, speed_step))
-    return terms
-
-
-def advanced(plan, blocks, row_samples, col_samples, head_samples, pace, trig):
-    speeds, spreads, time_step = pace
-    terms = speed_terms(plan, blocks)
-    results = []
-    for v, block in enumerate(blocks):
-        bends, across = bends_of(head_samples[v])
-        rate = terms[v] + limit_term(
-            bends, across, weno_eps * plan.step_h**2, turn_limit, plan.step_h
+    bends = [bend_of(at(k - 1), at(k), at(k + 1)) for k in range(count)]
+    weights = [sharp(bend, floor) for bend in bends]
+    bends = [zero] + bends + [zero]
+    weights = [zero + floor * floor] + weights + [zero + floor * floor]
+    return [
+        limit_term(
+            at(k + 1) - at(k - 1), bends[k : k + 3], weights[k : k + 3], accel_limit, speed_step
         )
-        rate = rate + drift_term(
-            row_samples[v], weno_eps * plan.step_y**2, speeds[v] * trig[1], spreads[1], plan.step_y
-        )
-        rate = rate + drift_term(
-            col_samples[v], weno_eps * plan.step_x**2, speeds[v] * trig[0], spreads[0], plan.step_x
-        )
-        results.append(block + time_step * jnp.minimum(rate, 0.0))
-    return results
-
-
-def step_kernel(plan, *refs):
+        for k in range(count)
+    ]
+
+
+class Terms:
+    def __init__(self, plan, offset, trig):
+        self.plan, self.trig = plan, trig
+        self.speeds, self.spreads, self.time_step = plan.pace(offset)
+        self.floor_x = weno_eps * plan.step_x**2
+        self.floor_y = weno_eps * plan.step_y**2
+        self.floor_h = weno_eps * plan.step_h**2
+
+    def set_trig(self):
+        for h in range(-2, self.plan.heads + 2):
+            self.trig[0, h + 2], self.trig[1, h + 2] = self.plan.trig(h)
+
+    def x(self, v, h, parts, cosine=None):
+        cosine = self.trig[0, h + 2] if cosine is None else cosine
+        return drift_term(*parts, self.speeds[v] * cosine, self.spreads[0], self.plan.step_x)
+
+    def y(self, v, h, parts, sine=None):
+        sine = self.trig[1, h + 2] if sine is None else sine
+        return drift_term(*parts, self.speeds[v] * sine, self.spreads[1], self.plan.step_y)
+
+    def heading(self, parts):
+        return limit_term(*parts, turn_limit, self.plan.step_h)
+
+    def heading_of(self, main, v, at):
+        blocks, bends, weights = main
+        return self.heading((
+            blocks[v, at + 1] - blocks[v, at - 1],
+            [bends[v, at + j] for j in (-1, 0, 1)],
+            [weights[v, at + j] for j in (-1, 0, 1)],
+        ))
+
+    def keep_bends(self, blocks, bends, weights, at, v):
+        bend = bend_of(blocks[v, at - 1], blocks[v, at], blocks[v, at + 1])
+        bends[v, at] = bend
+        weights[v, at] = sharp(bend, self.floor_h)
+
+    def step(self, block, rate):
+        return block + self.time_step * jnp.minimum(rate, 0.0)
+
+
+def early_kernel(plan, *refs):
     wide = plan.axes["ha"] > 2
-    names = ["value", "heads_even"] + (["heads_odd"] if wide else [])
-    names += ["ring", "corner_even"] + (["corner_odd"] if wide else [])
-    names += ["packed", "cols_even", "cols_odd", "failure", "offset", "out"]
-    names += ["f_a", "f_b", "x_a", "x_b", "s_a", "s_b", "x_s", "trig"]
+    names = ["value", "heads_even"] + (["heads_odd"] if wide else []) + ["ring", "offset"]
+    names += ["blocks", "rate_a", "rate_b", "bends", "weights", "trig"]
     r = dict(zip(names, refs, strict=True))
-    nv, heads, rows, cols = plan.speeds, plan.heads, plan.rows, plan.cols
-    heads_odd, corner_odd = r.get("heads_odd"), r.get("corner_odd")
-    pace = plan.pace(r["offset"])
+    nv, heads = plan.speeds, plan.heads
+    terms = Terms(plan, r["offset"], r["trig"])
+    terms.set_trig()
+    rows, columns = Shifts(plan, 0), Shifts(plan, 1)
+    blocks, ring = r["blocks"], r["ring"]
+    edge = edge_columns(plan)
+
+    def x_term(v, h, block):
+        term = terms.x(v, h, stencil(columns.turned(block), terms.floor_x))
+        return jnp.where(edge, 0.0, term)
+
+    for v in range(nv):
+        for h in range(-DEPTH, heads + DEPTH):
+            blocks[v, h + DEPTH] = head_block(
+                plan, r["value"], r["heads_even"], r.get("heads_odd"), v, h
+            )
+    kept = (blocks, r["bends"], r["weights"])
+
+    def bend_step(i, carry):
+        for v in range(nv):
+            terms.keep_bends(*kept, i, v)
+        return carry
+
+    lax.fori_loop(1, heads + 2 * DEPTH - 1, bend_step, 0)
+
+    def own_step(h, inner):
+        here = [blocks[v, h + DEPTH] for v in range(nv)]
+        outer = [ring[v, h] for v in range(nv)]
+        sums = [a + terms.heading_of(kept, v, h + DEPTH) for v, a in enumerate(speed_terms(here))]
+        outer_sums = speed_terms(outer)
+        for v in range(nv):
+            near = rows.near(here[v], outer[v], terms.floor_y)
+            outer_near = rows.near(outer[v], here[v], terms.floor_y)
+            parts = rows.stencil(near, *outer_near[1:])
+            outer_parts = rows.stencil(outer_near, *near[1:])
+            r["rate_a"][v, h + 2] = sums[v] + terms.y(v, h, parts) + x_term(v, h, here[v])
+            rate = outer_sums[v] + terms.y(v, h, outer_parts) + x_term(v, h, outer[v])
+            if inner:
+                samples = [ring[v, h + j] for j in range(-2, 3)]
+                rate = rate + terms.heading(stencil(samples, terms.floor_h))
+            r["rate_b"][v, h] = rate
+
+    def inner_step(h, carry):
+        own_step(h, True)
+        return carry
+
+    def outer_step(i, carry):
+        own_step(edge_of(plan, i, 0), False)
+        return carry
+
+    def face_step(i, carry):
+        h = edge_of(plan, i, 2)
+        here = [blocks[v, h + DEPTH] for v in range(nv)]
+        for v, term in enumerate(speed_terms(here)):
+            rate = term + terms.heading_of(kept, v, h + DEPTH)
+            r["rate_a"][v, h + 2] = rate + x_term(v, h, here[v])
+        return carry
+
+    lax.fori_loop(2, heads - 2, inner_step, 0)
+    lax.fori_loop(0, 4, outer_step, 0)
+    lax.fori_loop(0, 4, face_step, 0)
+
+
+def edge_columns(plan):
+    col = iota(plan, 1)
+    return jnp.logical_or(col < 2, col >= plan.cols - 2)
+
+
+def edge_of(plan, i, out):
+    return jnp.where(i < 2, i - out, plan.heads - 4 + i + out)
+
+
+def late_kernel(plan, *refs):
+    wide = plan.axes["ha"] > 2
+    names = ["blocks", "ring", "rate_a", "rate_b", "corner_even"]
+    names += (["corner_odd"] if wide else []) + ["packed", "cols_even", "cols_odd", "failure"]
+    names += ["offset", "out", "f_b", "s_a", "s_b", "x_s", "bends", "weights", "trig"]
+    r = dict(zip(names, refs, strict=True))
+    nv, heads, cols = plan.speeds, plan.heads, plan.cols
+    terms = Terms(plan, r["offset"], r["trig"])
+    terms.set_trig()
+    rows, columns = Shifts(plan, 0), Shifts(plan, 1)
     row, col = iota(plan, 0), iota(plan, 1)
-    lower = col % SLOT < DEPTH
+    blocks, f_b, s_a, s_b, x_s = r["blocks"], r["f_b"], r["s_a"], r["s_b"], r["x_s"]
+    edge_terms = {}
+    place = col % SLOT
+    lower = place < DEPTH
+    beyond = jnp.logical_or(
+        jnp.logical_and(lower, is_first("gx")),
+        jnp.logical_and(jnp.logical_not(lower), is_last("gx")),
+    )
     row_first = jnp.logical_and(row >= DEPTH, is_first("gy"))
     row_last = jnp.logical_and(row < DEPTH, is_last("gy"))
-    col_first = jnp.logical_and(col >= cols // 2, is_first("gx"))
-    col_last = jnp.logical_and(col < cols // 2, is_last("gx"))
-    f_a, f_b, x_a, x_b = r["f_a"], r["f_b"], r["x_a"], r["x_b"]
-    s_a, s_b, x_s = r["s_a"], r["s_b"], r["x_s"]
-
-    cos_lanes = jnp.zeros((rows, cols), jnp.float32)
-    sin_lanes = jnp.zeros((rows, cols), jnp.float32)
+    shift = lambda block, lanes: pltpu.roll(block, lanes % cols, 1)
+
+    def clamped(around, own):
+        near = jnp.where(place == 3, shift(own, -1), shift(own, -2))
+        far = jnp.where(place == 4, shift(own, 1), shift(own, 2))
+        return jnp.where(beyond, jnp.where(lower, near, far), around)
+
+    def faces_of(around, own):
+        return jnp.where(lower, around, own), jnp.where(lower, own, around)
+
+    def turned(packed, h):
+        return pltpu.roll(packed, cols - DEPTH - SLOT * (h + 2), 1)
+
+    edge = edge_columns(plan)
+
+    def edge_term(v, h, part):
+        return jnp.where(edge, turned(edge_terms[v, part], h), 0.0)
+
+    cos_lanes = jnp.zeros((plan.rows, cols), jnp.float32)
+    sin_lanes = jnp.zeros((plan.rows, cols), jnp.float32)
     for h in range(-2, heads + 2):
-        cosine, sine = plan.trig(h)
-        r["trig"][0, h + 2] = cosine
-        r["trig"][1, h + 2] = sine
-        cos_lanes = jnp.where(col // SLOT == h + 2, cosine, cos_lanes)
-        sin_lanes = jnp.where(col // SLOT == h + 2, sine, sin_lanes)
-
-    around = []
+        cos_lanes = jnp.where(col // SLOT == h + 2, terms.trig[0, h + 2], cos_lanes)
+        sin_lanes = jnp.where(col // SLOT == h + 2, terms.trig[1, h + 2], sin_lanes)
+
+    is_even = lax.axis_index("gx") % 2 == 0
+    faces = [[], []]
     for v in range(nv):
-        for h in range(-DEPTH, heads + DEPTH):
-            f_a[v, h + DEPTH] = head_block(plan, r["value"], r["heads_even"], heads_odd, v, h)
         for h in range(heads):
             f_b[v, h + 2] = r["ring"][v, h]
         for side in range(2):
             tile = r["corner_even"][v, 1 - side]
-            if corner_odd is not None:
-                tile = by_side("ha", tile, corner_odd[v, 1 - side])[side]
+            if wide:
+                tile = by_side("ha", tile, r["corner_odd"][v, 1 - side])[side]
             base = heads + 2 if side else 0
             f_b[v, base] = tile
             f_b[v, base + 1] = pltpu.roll(tile, DEPTH, 0)
-        pair = []
-        for part in range(2):
-            before, after = by_side("gx", r["cols_even"][v, part], r["cols_odd"][v, part])
-            pair.append(jnp.where(lower, before, after))
-        around.append(pair)
-        for h in range(-2, heads + 2):
-            slot = h + 2
-            ring = pltpu.roll(pair[0], cols - DEPTH - SLOT * slot, 1)
-            x_a[v, slot] = clamp_cols(plan, f_a[v, h + DEPTH], ring, col_first, col_last)
+        even, odd = r["cols_even"][v], r["cols_odd"][v]
+        before, after = jnp.where(is_even, odd, even), jnp.where(is_even, even, odd)
+        main = jnp.where(lower, before, shift(after, DEPTH))
+        outer = jnp.where(lower, shift(before, -DEPTH), after)
+        for part, around in ((0, main), (1, outer)):
+            own = r["packed"][v, part]
+            pair = faces_of(clamped(around, own), own)
+            x_terms = [
+                terms.x(v, 0, stencil(columns.turned(face), terms.floor_x), cos_lanes)
+                for face in pair
+            ]
+            edge_terms[v, part] = jnp.where(lower, x_terms[1], x_terms[0])
+            for side in range(2):
+                faces[side].append((pair[side], x_terms[side]))
+
+    for h in range(-2, heads + 2):
+        for v in range(nv):
+            block = blocks[v, h + DEPTH]
+            rate = r["rate_a"][v, h + 2] + edge_term(v, h, 0)
+            if not 0 <= h < heads:
+                samples = rows.samples(block, f_b[v, h + 2])
+                rate = rate + terms.y(v, h, stencil(samples, terms.floor_y))
+            s_a[v, h + 2] = terms.step(block, rate)
+    for h in range(heads):
+        for v in range(nv):
+            block = f_b[v, h + 2]
+            rate = r["rate_b"][v, h] + edge_term(v, h, 1)
+            if not 2 <= h < heads - 2:
+                samples = [f_b[v, h + 2 + j] for j in range(-2, 3)]
+                rate = rate + terms.heading(stencil(samples, terms.floor_h))
+            s_b[v, h] = terms.step(block, rate)
+
+    stepped = [[], []]
+    for side in range(2):
+        mains = [faces[side][2 * v] for v in range(nv)]
+        rings = [faces[side][2 * v + 1] for v in range(nv)]
+        sums = speed_terms([main for main, _ in mains])
+        for v, (block, x_term) in enumerate(mains):
+            samples = rows.samples(block, rings[v][0])
+            rate = sums[v] + x_term + terms.y(v, 0, stencil(samples, terms.floor_y), sin_lanes)
+            samples = columns.turned(block, SLOT)
+            rate = rate + terms.heading(stencil(samples, terms.floor_h))
+            stepped[side].append(terms.step(block, rate))
+
+    slot_id = col // SLOT
+    for v in range(nv):
+        own = jnp.zeros((plan.rows, cols), jnp.float32)
         for h in range(heads):
-            slot = h + 2
-            ring = pltpu.roll(pair[1], cols - DEPTH - SLOT * slot, 1)
-            x_b[v, h] = clamp_cols(plan, f_b[v, slot], ring, col_first, col_last)
-
-    def block_step(h, main, ring, row_of, x_of, base, store):
-        blocks = [main[v, h + base] for v in range(nv)]
-        heads_near = [[main[v, h + base + j] for j in range(-2, 3)] for v in range(nv)]
-        rows_near = [
-            ring_samples(blocks[v], ring[v, row_of(h)], row, 0, rows) for v in range(nv)
-        ]
-        cols_near = [ring_samples(blocks[v], x_of(v, h), col, 1, cols) for v in range(nv)]
-        trig = (r["trig"][0, h + 2], r["trig"][1, h + 2])
-        results = advanced(plan, blocks, rows_near, cols_near, heads_near, pace, trig)
+            block = s_a[v, h + 2]
+            own = jnp.where(slot_id == h + 2, shift(block, DEPTH + SLOT * (h + 2)), own)
+            s_b[v, h] = clamp_rows(plan, block, s_b[v, h], row_first, row_last)
+        around = clamped(jnp.where(lower, stepped[0][v], stepped[1][v]), own)
+        for h in range(heads):
+            x_s[v, h] = turned(around, h)
+
+    kept = (s_a, r["bends"], r["weights"])
+
+    def bend_step(i, carry):
         for v in range(nv):
-            store(v, h, results[v])
-
-    def put_a(v, h, block):
-        s_a[v, h + 2] = block
-
-    def put_b(v, h, block):
-        s_b[v, h] = block
-
-    def first_a(i, carry):
-        block_step(i - 2, f_a, f_b, lambda h: h + 2, lambda v, h: x_a[v, h + 2], DEPTH, put_a)
+            terms.keep_bends(*kept, i, v)
         return carry
 
-    def first_b(h, carry):
-        block_step(h, f_b, f_a, lambda h: h + DEPTH, lambda v, h: x_b[v, h], 2, put_b)
-        return carry
-
-    lax.fori_loop(0, heads + 4, first_a, 0)
-    lax.fori_loop(0, heads, first_b, 0)
-
-    faces = []
-    for keep_own in (jnp.logical_not(lower), lower):
-        mains = [jnp.where(keep_own, r["packed"][v, 0], around[v][0]) for v in range(nv)]
-        rings = [jnp.where(keep_own, r["packed"][v, 1], around[v][1]) for v in range(nv)]
-        rows_near = [ring_samples(mains[v], rings[v], row, 0, rows) for v in range(nv)]
-        shift = lambda block, lanes: pltpu.roll(block, lanes % cols, 1)
-        cols_near = [[shift(mains[v], -j) for j in (-2, -1)] + [mains[v]] for v in range(nv)]
-        cols_near = [near + [shift(near[2], -j) for j in (1, 2)] for near in cols_near]
-        heads_near = [
-            [mains[v] if j == 0 else shift(mains[v], -SLOT * j) for j in range(-2, 3)]
-            for v in range(nv)
-        ]
-        trig = (cos_lanes, sin_lanes)
-        faces.append(advanced(plan, mains, rows_near, cols_near, heads_near, pace, trig))
-
-    for v in range(nv):
-        both = jnp.where(lower, faces[0][v], faces[1][v])
-        for h in range(heads):
-            own = s_a[v, h + 2]
-            ring = pltpu.roll(both, cols - DEPTH - SLOT * (h + 2), 1)
-            x_s[v, h] = clamp_cols(plan, own, ring, col_first, col_last)
-            s_b[v, h] = clamp_rows(plan, own, s_b[v, h], row_first, row_last)
-
-    def put_out(v, h, block):
-        half = 0.5 * (r["value"][v, h] + block)
-        r["out"][v, h] = jnp.minimum(half, r["failure"][h])
+    lax.fori_loop(1, heads + 3, bend_step, 0)
 
     def second(h, carry):
-        block_step(h, s_a, s_b, lambda h: h, lambda v, h: x_s[v, h], 2, put_out)
+        here = [s_a[v, h + 2] for v in range(nv)]
+        sums = speed_terms(here)
+        for v, block in enumerate(here):
+            samples = columns.samples(block, x_s[v, h])
+            rate = terms.x(v, h, stencil(samples, terms.floor_x))
+            rate = rate + sums[v] + terms.heading_of(kept, v, h + 2)
+            samples = rows.samples(block, s_b[v, h])
+            rate = rate + terms.y(v, h, stencil(samples, terms.floor_y))
+            half = 0.5 * (blocks[v, h + DEPTH] + terms.step(block, rate))
+            r["out"][v, h] = jnp.minimum(half, r["failure"][h])
         return carry
 
     lax.fori_loop(0, heads, second, 0)
@@ -444,24 +589,33 @@
     )
     corners = turn_swaps(corner)
     pack = pack_cols if wide else pack_cols_narrow
-    (packed,) = call(
-        pack, plan, [(nv, 2) + tile], [value, *beside, ring], "v" * (2 + len(beside))
+    packed, even_cols, odd_cols = call(
+        pack,
+        plan,
+        [(nv, 2) + tile, (nv,) + tile, (nv,) + tile],
+        [value, *beside, ring],
+        "v" * (2 + len(beside)),
     )
-    even_cols = swap(packed, "gx", False)
-    odd_cols = swap(packed, "gx", True)
-    args = [value, *beside, ring, *corners, packed, even_cols, odd_cols, failure]
-    scratch = [
-        pltpu.VMEM((nv, heads + 2 * DEPTH) + tile, jnp.float32),
-        pltpu.VMEM((nv, heads + 4) + tile, jnp.float32),
-        pltpu.VMEM((nv, heads + 4) + tile, jnp.float32),
-        pltpu.VMEM((nv, heads) + tile, jnp.float32),
-        pltpu.VMEM((nv, heads + 4) + tile, jnp.float32),
-        pltpu.VMEM((nv, heads) + tile, jnp.float32),
-        pltpu.VMEM((nv, heads) + tile, jnp.float32),
-        pltpu.SMEM((2, heads + 4), jnp.float32),
-    ]
+    even_cols = swap(even_cols, "gx", False)
+    odd_cols = swap(odd_cols, "gx", True)
+    deep = (nv, heads + 2 * DEPTH) + tile
+    edged = (nv, heads + 4) + tile
+    memory = lambda shape: pltpu.VMEM(shape, jnp.float32)
+    trig = pltpu.SMEM((2, heads + 4), jnp.float32)
+    blocks, rate_a, rate_b = call(
+        early_kernel,
+        plan,
+        [deep, edged, value.shape],
+        [value, *beside, ring, speed_offset],
+        "v" * (2 + len(beside)) + "s",
+        [memory(deep), memory(deep), trig],
+        flops=50000000,
+    )
+    args = [blocks, ring, rate_a, rate_b, *corners, packed, even_cols, odd_cols, failure]
+    scratch = [memory(edged), memory(edged), memory(value.shape), memory(value.shape)]
+    scratch += [memory(edged), memory(edged), trig]
     (out,) = call(
-        step_kernel,
+        late_kernel,
         plan,
         [value.shape],
         args + [speed_offset],
@@ -472,8 +626,8 @@
     return out
 
 
-def pack_cols_narrow(plan, value, heads_even, ring, packed_out):
-    pack_cols(plan, value, heads_even, None, ring, packed_out)
+def pack_cols_narrow(plan, value, heads_even, *rest):
+    pack_cols(plan, value, heads_even, None, *rest)
 
 
 def solution(mesh):

time: 17.9 us -> 15.7 us (0.88)
  waiting for transfers between devices: 2.79 us -> 0.77 us
  Pallas kernels: 6.13 us -> 5.87 us
    ppermute x5, waiting for transfers between devices: 2.1 us -> 0.08 us  [swap(): return lax.ppermute(payload, axis, pairs + [(j, i) for i, j in pairs])]
    pallas_call x5 -> x6, Pallas kernels: 6.13 us -> 5.87 us  [call(): pl.pallas_call(functools.partial(body, plan), out_shape=[jax.ShapeDtypeSt...]
  transfers between devices with their start and end apart: 6 -> 6, of which waited for: 2 -> 2; matrix products, arithmetic and copies ran while one was open for 0% -> 0% of each run, Pallas kernels for 9% -> 23%
where the time goes in v3:
time: 15.7 us; the launch traced here: 15.5 us
  starting transfers between devices  6.51 us (41%)
  Pallas kernels  5.87 us (37%)
  between operations  1.4 us (9%)
  local copies, waits for them, and re-layouts  0.95 us (6%)
  waiting for transfers between devices  0.77 us (5%)
    ppermute x5, starting transfers between devices, swap(): return lax.ppermute(payload, axis, pairs + [(j, i) for i, j in pairs])  6.5 us
    pallas_call x6, Pallas kernels, call(): pl.pallas_call(functools.partial(body, plan), out_shape=[jax.ShapeDtypeSt...  5.87 us
    unnamed x8, local copies, waits for them, and re-layouts  0.95 us
    ppermute x1, waiting for transfers between devices, swap(): return lax.ppermute(payload, ('gx', axis), pairs)  0.69 us
  transfers between devices with their start and end apart: 6, of which 2 were waited for; matrix products, arithmetic and copies ran while one was open for 0% of the time, Pallas kernels for 23%

profile of v3, /device:TPU:17, one launch (start us, length us, event | category | flops | bytes accessed | tf_op | source)
XLA Modules:
  0.0 15.5 jit_solution(3292697942566234179)
XLA Ops:
  0.0 1.2 %collective-permute-start = (f32[4,8,8,128]{3,2,1,0:T(8,128)}, f32[4,8,8,128]{3,2,1,0:T(8,128)S(1)}, u32[]{:S(2)}, u32[]{:S(2)}) collective-permute-start(f32[4,8,8,128]{3,2,1,0:T(8,128)} %value.5), channel_id=1, source_target_pairs={{0,1},{1,0},{2,3},{3,2},{4,5},{5,4},{6,7},{7,6},{8,9},{9,8},{10,11... | collective-permute-start | bytes 393224 | tf_op jit(solution)/shard_map/ppermute | solution.py:76
  1.2 0.0 copy-start
  1.2 0.9 %copy-done = f32[4,8,8,128]{3,2,1,0:T(8,128)S(1)} copy-done((f32[4,8,8,128]{3,2,1,0:T(8,128)S(1)}, f32[4,8,8,128]{3,2,1,0:T(8,128)}, u32[]{:S(2)}) %copy-start) | copy-done | bytes 131096
  2.2 0.0 copy-start.1
  2.2 0.0 copy-start.2
  2.2 1.4 %collective-permute-start.1 = (f32[4,4,8,128]{3,2,1,0:T(8,128)S(1)}, f32[4,4,8,128]{3,2,1,0:T(8,128)S(1)}, u32[]{:S(2)}, u32[]{:S(2)}) collective-permute-start(f32[4,4,8,128]{3,2,1,0:T(8,128)S(1)} %get-tuple-element.15), channel_id=1, source_target_pairs={{0,2},{4,6},{2,0},{6,4},{1,3},{5,7},{3,1},{7,5},{8,10},{12,14},{10... | collective-permute-start | bytes 196616 | tf_op jit(solution)/shard_map/ppermute | solution.py:76
  3.6 0.0 collective-permute-start.2
  4.2 0.0 copy-start.3
  4.9 0.0 copy-done.2
  4.9 0.0 copy-done.3
  4.9 1.4 %failure_field.1._.refs_8_ = f32[8,8,128]{2,1,0:T(8,128)S(1)} custom-call(f32[5,128]{1,0:T(8,128)S(1)} %copy-done.2, s32[2,16]{1,0:T(2,128)S(1)} %copy-done.3, f32[1]{0:T(128)S(6)} %copy.6.horizon, s32[1]{0:T(128)S(6)} %copy.7.offset.refs_3_.refs_9_), custom_call_target="tpu_custom_call" | custom-call | flops 1000000 | bytes 400000 | tf_op jit(solution)/shard_map/failure_field/pallas_call | solution.py:101
  6.3 0.0 collective-permute-done.1.even_in
  6.3 0.7 %collective-permute-done.2.odd_in = f32[4,4,8,128]{3,2,1,0:T(8,128)S(1)} collective-permute-done((f32[4,4,8,128]{3,2,1,0:T(8,128)S(1)}, f32[4,4,8,128]{3,2,1,0:T(8,128)S(1)}, u32[]{:S(2)}, u32[]{:S(2)}) %collective-permute-start.2) | collective-permute-done | bytes 65568 | tf_op jit(solution)/shard_map/ppermute | solution.py:83
  7.0 0.0 copy-done.1
  7.0 0.3 %collective-permute-start.3 = (f32[4,2,8,128]{3,2,1,0:T(8,128)S(1)}, f32[4,2,8,128]{3,2,1,0:T(8,128)S(1)}, u32[]{:S(2)}, u32[]{:S(2)}) collective-permute-start(f32[4,2,8,128]{3,2,1,0:T(8,128)S(1)} %get-tuple-element.21), channel_id=1, source_target_pairs={{0,1},{1,0},{2,3},{3,2},{4,5},{5,4},{6,7},{7,6},{8,9},{9,8},{10,11... | collective-permute-start | bytes 98312 | tf_op jit(solution)/shard_map/ppermute | solution.py:76
  7.3 0.0 collective-permute-done.refs_1_.heads_even
  7.3 0.2 %pack_cols_narrow.1 = (f32[4,2,8,128]{3,2,1,0:T(8,128)S(1)}, f32[4,8,128]{2,1,0:T(8,128)S(1)}, f32[4,8,128]{2,1,0:T(8,128)S(1)}) custom-call(f32[4,8,8,128]{3,2,1,0:T(8,128)S(1)} %copy-done.1, f32[4,8,8,128]{3,2,1,0:T(8,128)S(1)} %collective-permute-done.refs_1_.heads_even, f32[4,8,8,128]{3,2,1,0:T(8,128)S(1)} %get-tuple-element.17.refs_2_.rest_0_.refs_1_), custom_call_target="tpu_custom_call" | custom-call | flops 1000000 | bytes 400000 | tf_op jit(solution)/shard_map/pack_cols_narrow/pallas_call | solution.py:101
  7.6 2.4 %collective-permute-start.4 = (f32[4,8,128]{2,1,0:T(8,128)S(1)}, f32[4,8,128]{2,1,0:T(8,128)S(1)}, u32[]{:S(2)}, u32[]{:S(2)}) collective-permute-start(f32[4,8,128]{2,1,0:T(8,128)S(1)} %get-tuple-element.23), channel_id=1, source_target_pairs={{0,8},{16,24},{8,0},{24,16},{1,9},{17,25},{9,1},{25,17},{2,10},{18... | collective-permute-start | bytes 49160 | tf_op jit(solution)/shard_map/ppermute | solution.py:76
  10.0 1.2 %collective-permute-start.5 = (f32[4,8,128]{2,1,0:T(8,128)S(1)}, f32[4,8,128]{2,1,0:T(8,128)S(1)}, u32[]{:S(2)}, u32[]{:S(2)}) collective-permute-start(f32[4,8,128]{2,1,0:T(8,128)S(1)} %get-tuple-element.24), channel_id=1, source_target_pairs={{8,16},{24,0},{16,8},{0,24},{9,17},{25,1},{17,9},{1,25},{10,18},{2... | collective-permute-start | bytes 49160 | tf_op jit(solution)/shard_map/ppermute | solution.py:76
  11.2 1.9 %early_kernel.1 = (f32[4,16,8,128]{3,2,1,0:T(8,128)S(1)}, f32[4,12,8,128]{3,2,1,0:T(8,128)S(1)}, f32[4,8,8,128]{3,2,1,0:T(8,128)S(1)}) custom-call(f32[4,8,8,128]{3,2,1,0:T(8,128)S(1)} %copy-done.1, f32[4,8,8,128]{3,2,1,0:T(8,128)S(1)} %collective-permute-done.refs_1_.heads_even, f32[4,8,8,128]{3,2,1,0:T(8,128)S(1)} %get-tuple-element.17.refs_2_.rest_0_.refs_1_, ...), custom_call_target="tpu_custom_call" | custom-call | flops 50000000 | bytes 400000 | tf_op jit(solution)/shard_map/early_kernel/pallas_call | solution.py:101
  13.0 0.0 collective-permute-done.3.refs_4_
  13.1 0.0 collective-permute-done.4.refs_6_
  13.1 0.1 collective-permute-done.5.refs_7_
  13.1 2.4 %late_kernel.1 = f32[4,8,8,128]{3,2,1,0:T(8,128)} custom-call(f32[4,16,8,128]{3,2,1,0:T(8,128)S(1)} %get-tuple-element.18.refs_0_, f32[4,8,8,128]{3,2,1,0:T(8,128)S(1)} %get-tuple-element.17.refs_2_.rest_0_.refs_1_, f32[4,12,8,128]{3,2,1,0:T(8,128)S(1)} %get-tuple-element.19.refs_2_, f32[4,8,8,128]{3,2,1,0:T(8,128)S(1)} %get-tuple-element.20.refs_3_, ...), custom_call_target="tpu_custom_call" | custom-call | flops 100000000 | bytes 400000 | tf_op jit(solution)/shard_map/late_kernel/pallas_call | solution.py:101
  (2 shorter events, 0.1 us)
Async XLA Ops:
  0.0 7.3 %collective-permute-start = (f32[4,8,8,128]{3,2,1,0:T(8,128)}, f32[4,8,8,128]{3,2,1,0:T(8,128)S(1)}, u32[]{:S(2)}, u32[]{:S(2)}) collective-permute-start(f32[4,8,8,128]{3,2,1,0:T(8,128)} %value.5), channel_id=1, source_target_pairs={{0,1},{1,0},{2,3},{3,2},{4,5},{5,4},{6,7},{7,6},{8,9},{9,8},{10,11... | collective-permute-start | bytes 393224 | tf_op jit(solution)/shard_map/ppermute | solution.py:76
  1.2 0.9 %copy-start = (f32[4,8,8,128]{3,2,1,0:T(8,128)S(1)}, f32[4,8,8,128]{3,2,1,0:T(8,128)}, u32[]{:S(2)}) copy-start(f32[4,8,8,128]{3,2,1,0:T(8,128)} %value.5) | copy-start | bytes 393220
  2.2 4.8 %copy-start.1 = (f32[4,8,8,128]{3,2,1,0:T(8,128)S(1)}, f32[4,8,8,128]{3,2,1,0:T(8,128)}, u32[]{:S(2)}) copy-start(f32[4,8,8,128]{3,2,1,0:T(8,128)} %value.5) | copy-start | bytes 393220
  2.2 2.7 %copy-start.2 = (f32[5,128]{1,0:T(8,128)S(1)}, f32[5,128]{1,0:T(8,128)}, u32[]{:S(2)}) copy-start(f32[5,128]{1,0:T(8,128)} %obstacles.1) | copy-start | bytes 7684
  2.2 4.1 %collective-permute-start.1 = (f32[4,4,8,128]{3,2,1,0:T(8,128)S(1)}, f32[4,4,8,128]{3,2,1,0:T(8,128)S(1)}, u32[]{:S(2)}, u32[]{:S(2)}) collective-permute-start(f32[4,4,8,128]{3,2,1,0:T(8,128)S(1)} %get-tuple-element.15), channel_id=1, source_target_pairs={{0,2},{4,6},{2,0},{6,4},{1,3},{5,7},{3,1},{7,5},{8,10},{12,14},{10... | collective-permute-start | bytes 196616 | tf_op jit(solution)/shard_map/ppermute | solution.py:76
  3.6 3.4 %collective-permute-start.2 = (f32[4,4,8,128]{3,2,1,0:T(8,128)S(1)}, f32[4,4,8,128]{3,2,1,0:T(8,128)S(1)}, u32[]{:S(2)}, u32[]{:S(2)}) collective-permute-start(f32[4,4,8,128]{3,2,1,0:T(8,128)S(1)} %get-tuple-element.16), channel_id=1, source_target_pairs={{0,8},{2,4},{4,2},{6,14},{8,0},{10,12},{12,10},{14,6},{16,24},{18,... | collective-permute-start | bytes 196616 | tf_op jit(solution)/shard_map/ppermute | solution.py:83
  4.2 0.7 %copy-start.3 = (s32[2,16]{1,0:T(2,128)S(1)}, s32[2,16]{1,0:T(2,128)}, u32[]{:S(2)}) copy-start(s32[2,16]{1,0:T(2,128)} %slots.1) | copy-start | bytes 388
  7.0 6.0 %collective-permute-start.3 = (f32[4,2,8,128]{3,2,1,0:T(8,128)S(1)}, f32[4,2,8,128]{3,2,1,0:T(8,128)S(1)}, u32[]{:S(2)}, u32[]{:S(2)}) collective-permute-start(f32[4,2,8,128]{3,2,1,0:T(8,128)S(1)} %get-tuple-element.21), channel_id=1, source_target_pairs={{0,1},{1,0},{2,3},{3,2},{4,5},{5,4},{6,7},{7,6},{8,9},{9,8},{10,11... | collective-permute-start | bytes 98312 | tf_op jit(solution)/shard_map/ppermute | solution.py:76
  7.6 5.5 %collective-permute-start.4 = (f32[4,8,128]{2,1,0:T(8,128)S(1)}, f32[4,8,128]{2,1,0:T(8,128)S(1)}, u32[]{:S(2)}, u32[]{:S(2)}) collective-permute-start(f32[4,8,128]{2,1,0:T(8,128)S(1)} %get-tuple-element.23), channel_id=1, source_target_pairs={{0,8},{16,24},{8,0},{24,16},{1,9},{17,25},{9,1},{25,17},{2,10},{18... | collective-permute-start | bytes 49160 | tf_op jit(solution)/shard_map/ppermute | solution.py:76
  10.0 3.2 %collective-permute-start.5 = (f32[4,8,128]{2,1,0:T(8,128)S(1)}, f32[4,8,128]{2,1,0:T(8,128)S(1)}, u32[]{:S(2)}, u32[]{:S(2)}) collective-permute-start(f32[4,8,128]{2,1,0:T(8,128)S(1)} %get-tuple-element.24), channel_id=1, source_target_pairs={{8,16},{24,0},{16,8},{0,24},{9,17},{25,1},{17,9},{1,25},{10,18},{2... | collective-permute-start | bytes 49160 | tf_op jit(solution)/shard_map/ppermute | solution.py:76
